TPU v7x, 32 devices: a whole 2x2x4 slice. The times are simulated.
32 devices in a mesh: dom: 8 (over z, x), rep: 4 (over y, core).
Axes of the slice: x: 2, y: 2, z: 4, core: 2. Of those that a mesh axis runs over, the one named last changes fastest.
Arguments:
- features: bfloat16 [2048, 256], P('dom'), may hold values from -6 to 6
- positions: float32 [3, 2048], P(None, 'dom'), may hold values from -6 to 6
- radial: bfloat16 [8, 256, 256], replicated, may hold values from -0.03125 to 0.03125
- mixing: bfloat16 [256, 256], replicated, may hold values from -0.375 to 0.375
- readout: float32 [256], replicated, may hold values from -4 to 4
- decay: float32 [8], replicated, may hold values from 0.1 to 1
- send_rows: int32 [4, 1024], P(None, 'dom'), may hold values from 0 to 255
- pair_home: int32 [1536], P(('dom', 'rep')), may hold values from 0 to 1
- pair_other: int32 [1536], P(('dom', 'rep')), may hold values from 0 to 5
- pair_kind: int32 [1536], P(('dom', 'rep')), may hold values from 0 to 7
- pair_image: int32 [3, 1536], P(None, ('dom', 'rep')), may hold values from -1 to 1
Outputs:
- grad_features: bfloat16 [2048, 256], P('dom')
- forces: float32 [3, 2048], P(None, 'dom')
- virials: float32 [6, 2048], P(None, 'dom')
- grad_mixing: float32 [256, 256], P('dom', 'rep')
Inputs may be any that keep to these rules, and one draw needn't show every extreme that they name: `send_rows`: rows may repeat within a round.
All inputs are finite; a program needn't handle non-finite values.
Results may differ from a plain program's by a relative error of at most 0.006.
Values may be sent and summed in bfloat16 or wider, within the bound.
A program may use at most 128 MiB of HBM per device.

v0:
```python
import jax
import jax.numpy as jnp
from jax import lax
from jax.sharding import PartitionSpec as P

TILE_ATOMS = 128


offsets = (1, -1, 2, -2)
cell_edge = 2.0
component_pairs = ((0, 0), (1, 1), (2, 2), (0, 1), (0, 2), (1, 2))
highest_precision = lax.Precision.HIGHEST


def from_behind(array, axis, by):
    count = lax.axis_size(axis)
    return lax.ppermute(array, axis, [(i, (i + by) % count) for i in range(count)])


def pair_setup(ext_feat, ext_pos, pair_home, pair_other, pair_kind, pair_image, radial, decay):
    channel_count = ext_feat.shape[1]
    tiles_feat = ext_feat.reshape(-1, TILE_ATOMS, channel_count)
    tiles_pos = ext_pos.reshape(3, -1, TILE_ATOMS)
    far_end = (
        jnp.take(tiles_pos, pair_other, axis=1)
        + pair_image[:, :, None].astype(jnp.float32) * cell_edge
    )
    near_end = jnp.take(tiles_pos, pair_home, axis=1)
    separation = far_end[:, :, None, :] - near_end[:, :, :, None]
    kind_table = (pair_kind[:, None] == lax.iota(jnp.int32, decay.shape[0])[None, :]).astype(
        jnp.float32
    )
    rates = jnp.sum(kind_table * decay[None, :], axis=1)
    kernel = jnp.exp(-rates[:, None, None] * jnp.sum(separation * separation, axis=0))
    partner_rows = jnp.take(tiles_feat, pair_other, axis=0)
    chosen = jnp.take(radial, pair_kind, axis=0)
    mapped = jnp.einsum(
        "pbc,pcd->pbd", partner_rows, chosen, preferred_element_type=jnp.float32
    ).astype(jnp.bfloat16)
    return (separation, rates, kernel, mapped, chosen)


def atom_section(message, mixing, readout):
    packed = message.astype(jnp.bfloat16)
    mixed_rows = jnp.dot(packed, mixing, preferred_element_type=jnp.float32)
    sigmoid_rows = jax.nn.sigmoid(mixed_rows)
    slope_rows = (readout * sigmoid_rows * (1.0 + mixed_rows * (1.0 - sigmoid_rows))).astype(
        jnp.bfloat16
    )
    adjoint = lax.dot_general(
        slope_rows, mixing, (((1,), (1,)), ((), ())), preferred_element_type=jnp.float32
    ).astype(jnp.bfloat16)
    return (packed, slope_rows, adjoint)


def on_device(
    features,
    positions,
    radial,
    mixing,
    readout,
    decay,
    send_rows,
    pair_home,
    pair_other,
    pair_kind,
    pair_image,
):
    count_of_atoms, channel_count = features.shape
    home_tiles = count_of_atoms // TILE_ATOMS
    extended_tiles = home_tiles + len(offsets)
    halo_feat = []
    halo_pos = []
    for section_no in range(len(offsets)):
        picked_feat = jnp.take(features, send_rows[section_no], axis=0)
        picked_pos = jnp.take(positions, send_rows[section_no], axis=1)
        halo_feat.append(from_behind(picked_feat, "dom", offsets[section_no]))
        halo_pos.append(from_behind(picked_pos, "dom", offsets[section_no]))
    ext_feat = jnp.concatenate([features] + halo_feat, axis=0)
    ext_pos = jnp.concatenate([positions] + halo_pos, axis=1)
    separation, rates, kernel, mapped, chosen = pair_setup(
        ext_feat, ext_pos, pair_home, pair_other, pair_kind, pair_image, radial, decay
    )
    kernel_low = kernel.astype(jnp.bfloat16)
    message_rows = jnp.einsum(
        "pab,pbd->pad", kernel_low, mapped, preferred_element_type=jnp.float32
    )
    home_lookup_table = (pair_home[None, :] == lax.iota(jnp.int32, home_tiles)[:, None]).astype(
        jnp.float32
    )
    partner_table = (pair_other[None, :] == lax.iota(jnp.int32, extended_tiles)[:, None]).astype(
        jnp.float32
    )
    message_portion = jnp.einsum(
        "so,oxe->sxe", home_lookup_table, message_rows, precision=highest_precision
    ).reshape(count_of_atoms, channel_count)
    message = lax.psum(message_portion, "rep")
    packed, slope_rows, adjoint = atom_section(message, mixing, readout)
    column_share = channel_count // lax.axis_size("rep")
    column_start = lax.axis_index("rep") * column_share
    slope_cols = lax.dynamic_slice_in_dim(slope_rows, column_start, column_share, 1)
    mixing_part = lax.dot_general(
        packed, slope_cols, (((0,), (0,)), ((), ())), preferred_element_type=jnp.float32
    )
    grad_mixing = lax.psum_scatter(mixing_part, "dom", scatter_dimension=0, tiled=True)
    adjoint_tiles = jnp.take(
        adjoint.reshape(home_tiles, TILE_ATOMS, channel_count), pair_home, axis=0
    )
    kernel_grad = jnp.einsum(
        "pad,pbd->pab", adjoint_tiles, mapped, preferred_element_type=jnp.float32
    )
    mapped_grad = jnp.einsum(
        "pab,pad->pbd", kernel_low, adjoint_tiles, preferred_element_type=jnp.float32
    ).astype(jnp.bfloat16)
    feature_grad = jnp.einsum(
        "pbd,pcd->pbc", mapped_grad, chosen, preferred_element_type=jnp.float32
    )
    weight = -2.0 * rates[:, None, None] * kernel * kernel_grad
    home_atom_side = []
    partner_side = []
    for axis_one in range(3):
        pull = weight * separation[axis_one]
        home_atom_side.append(jnp.sum(pull, axis=2))
        partner_side.append(-jnp.sum(pull, axis=1))
    for axis_one, axis_two in component_pairs:
        product = weight * separation[axis_one] * separation[axis_two]
        home_atom_side.append(-0.5 * jnp.sum(product, axis=2))
        partner_side.append(-0.5 * jnp.sum(product, axis=1))
    home_atom_side = jnp.stack(home_atom_side)
    partner_side = jnp.stack(partner_side)
    ext_grad = jnp.einsum(
        "jp,pbc->jbc", partner_table, feature_grad, precision=highest_precision
    ).reshape(extended_tiles * TILE_ATOMS, channel_count)
    extended_side = jnp.einsum(
        "it,ztq->ziq", partner_table, partner_side, precision=highest_precision
    ).reshape(9, extended_tiles * TILE_ATOMS)
    self_side = (
        jnp.einsum(
            "qk,gkv->gqv", home_lookup_table, home_atom_side, precision=highest_precision
        ).reshape(9, count_of_atoms)
        + extended_side[:, :count_of_atoms]
    )
    own_grad = ext_grad[:count_of_atoms]
    atom_iota = lax.iota(jnp.int32, count_of_atoms)
    for section_no in range(len(offsets)):
        lower_row = count_of_atoms + section_no * TILE_ATOMS
        returned = (
            ext_grad[lower_row : lower_row + TILE_ATOMS],
            extended_side[:, lower_row : lower_row + TILE_ATOMS],
        )
        received = from_behind((returned[0], returned[1]), "dom", -offsets[section_no])
        send_onehot = (send_rows[section_no][:, None] == atom_iota[None, :]).astype(jnp.float32)
        own_grad = own_grad + jnp.einsum(
            "ta,tc->ac", send_onehot, received[0], precision=highest_precision
        )
        self_side = self_side + jnp.einsum(
            "ta,ct->ca", send_onehot, received[1], precision=highest_precision
        )
    totals = lax.psum((own_grad, self_side), "rep")
    grad_features = totals[0].astype(jnp.bfloat16)
    forces = totals[1][:3]
    virials = totals[1][3:]
    return (grad_features, forces, virials, grad_mixing)


def solution(mesh):
    in_specs = (
        P("dom", None),
        P(None, "dom"),
        P(),
        P(),
        P(),
        P(),
        P(None, "dom"),
        P(("dom", "rep")),
        P(("dom", "rep")),
        P(("dom", "rep")),
        P(None, ("dom", "rep")),
    )
    out_specs = (P("dom", None), P(None, "dom"), P(None, "dom"), P("dom", "rep"))
    return jax.shard_map(
        on_device, mesh=mesh, in_specs=in_specs, out_specs=out_specs, check_vma=False
    )
```

profile of v0, /device:TPU:1, one launch (start us, length us, event | category | flops | bytes accessed | tf_op | source)
XLA Modules:
  0.0 181.9 jit_solution(13780323286875646111)
XLA Ops:
  7.3 0.8 compare_and_fusion.2
  8.1 1.7 gather_fusion.12
  9.9 4.2 %collective-permute-start.7 = (bf16[128,256]{1,0:T(8,128)(2,1)S(1)}, bf16[128,256]{1,0:T(8,128)(2,1)S(1)}, u32[]{:S(2)}, u32[]{:S(2)}) collective-permute-start(bf16[128,256]{1,0:T(8,128)(2,1)S(1)} %broadcast_select_fusion.9), channel_id=1, source_target_pairs={{0,24},{4,28},{8,0},{12,4},{16,8},{20,12},{24,16},{28,20},{1,25},{... | collective-permute-start | bytes 196616 | tf_op jit(solution)/shard_map/ppermute | solution.py:17
  14.1 1.7 gather_fusion.11
  16.0 1.7 gather_fusion.10
  17.7 4.2 %collective-permute-start.5 = (bf16[128,256]{1,0:T(8,128)(2,1)S(1)}, bf16[128,256]{1,0:T(8,128)(2,1)S(1)}, u32[]{:S(2)}, u32[]{:S(2)}) collective-permute-start(bf16[128,256]{1,0:T(8,128)(2,1)S(1)} %broadcast_select_fusion.11), channel_id=1, source_target_pairs={{0,28},{4,0},{8,4},{12,8},{16,12},{20,16},{24,20},{28,24},{1,29},{... | collective-permute-start | bytes 196616 | tf_op jit(solution)/shard_map/ppermute | solution.py:17
  22.0 1.7 gather_fusion.9
  23.8 0.8 copy.36
  24.6 0.6 gather_fusion.3
  25.6 0.6 gather_fusion.6
  26.2 0.6 gather_fusion.5
  26.8 0.6 gather_fusion.4
  28.0 5.0 %gather_fusion.1 = bf16[48,256,256]{2,1,0:T(8,128)(2,1)} fusion(bf16[8,256,256]{2,1,0:T(8,128)(2,1)S(1)} %copy-done, s32[1024]{0:T(1024)S(1)} %get-tuple-element.74), kind=kCustom, calls=%fused_computation.11 | custom fusion | bytes 12583104 | tf_op jit(solution)/shard_map/jit(_take)/gather | solution.py:36
  33.0 4.1 %collective-permute-start.1 = (f32[3,128]{0,1:T(8,128)S(1)}, f32[3,128]{0,1:T(8,128)S(1)}, u32[]{:S(2)}, u32[]{:S(2)}) collective-permute-start(f32[3,128]{0,1:T(8,128)S(1)} %select_bitcast_fusion.3), channel_id=1, source_target_pairs={{0,28},{4,0},{8,4},{12,8},{16,12},{20,16},{24,20},{28,24},{1,29},{... | collective-permute-start | bytes 4616 | tf_op jit(solution)/shard_map/ppermute | solution.py:17
  37.2 1.3 collective-permute-done.1
  38.6 4.8 %collective-permute-done.2 = f32[3,128]{0,1:T(8,128)S(1)} collective-permute-done((f32[3,128]{0,1:T(8,128)S(1)}, f32[3,128]{0,1:T(8,128)S(1)}, u32[]{:S(2)}, u32[]{:S(2)}) %collective-permute-start.2) | collective-permute-done | bytes 1568 | tf_op jit(solution)/shard_map/ppermute | solution.py:17
  43.7 3.5 %collective-permute-done.3 = f32[3,128]{0,1:T(8,128)S(1)} collective-permute-done((f32[3,128]{0,1:T(8,128)S(1)}, f32[3,128]{0,1:T(8,128)S(1)}, u32[]{:S(2)}, u32[]{:S(2)}) %collective-permute-start.3) | collective-permute-done | bytes 1568 | tf_op jit(solution)/shard_map/ppermute | solution.py:17
  47.3 0.7 gather_fusion.8
  48.1 0.6 gather_fusion.7
  48.9 7.5 %broadcast_subtract_fusion = (f32[3,48,128,128]{3,2,1,0:T(8,128)}, f32[48,128,128]{2,1,0:T(8,128)}) fusion(f32[3,48,128]{2,1,0:T(8,128)S(1)} %copy.46, f32[3,48,128]{2,1,0:T(8,128)S(1)} %copy.45), kind=kLoop, calls=%fused_computation.19 | loop fusion | flops 6291456 | bytes 12730368 | tf_op jit(solution)/shard_map/sub | solution.py:29
  56.4 2.5 %gather_fusion = bf16[48,128,256]{2,1,0:T(8,128)(2,1)} fusion(bf16[6,128,256]{2,1,0:T(8,128)(2,1)S(1)} %bitcast.172, s32[1024]{0:T(1024)S(1)} %get-tuple-element.75), kind=kCustom, calls=%fused_computation.10 | custom fusion | bytes 6291648 | tf_op jit(solution)/shard_map/jit(_take)/gather | solution.py:35
  59.0 5.2 %fusion.21 = bf16[48,128,256]{2,1,0:T(8,128)(2,1)S(1)} fusion(bf16[48,256,256]{2,1,0:T(8,128)(2,1)} %gather_fusion.1, pred[48]{0:T(512)(128)(4,1)S(1)} %get-tuple-element.77, bf16[48,128,256]{2,1,0:T(8,128)(2,1)} %gather_fusion, pred[48]{0:T(512)(128)(4,1)S(1)} %get-tuple-element.76), kind=kOutput, calls=%fused_computation.42 | convolution fusion | flops 811597824 | bytes 12583008 | tf_op jit(solution)/shard_map/pbc,pcd->pbd/dot_general | solution.py:37
  64.2 1.0 fusion.80
  65.3 0.7 copy-done.3
  66.0 5.7 %fusion.2 = f32[2,128,256]{2,0,1:T(2,128)S(1)} fusion(f32[48,128,256]{2,1,0:T(8,128)S(1)} %fusion.80, s32[48]{0:T(128)S(1)} %copy-done.9), kind=kOutput, calls=%fused_computation.16 | convolution fusion | flops 37748832 | bytes 6553792 | tf_op jit(solution)/shard_map/so,oxe->sxe/dot_general | solution.py:94
  71.6 17.6 %all-reduce.3 = bf16[256,256]{1,0:T(8,128)(2,1)S(1)} all-reduce(f32[256,256]{1,0:T(8,128)S(1)} %bitcast.175), channel_id=1, replica_groups=mesh['dom'=8,'rep'=4] {'rep'}, use_global_device_ids=true, to_apply=%region_2.6 | all-reduce | flops 65536 | bytes 393216 | tf_op jit(solution)/shard_map/psum | solution.py:97
  89.8 2.6 %gather_fusion.2 = bf16[48,128,256]{2,1,0:T(8,128)(2,1)} fusion(bf16[2,128,256]{2,1,0:T(8,128)(2,1)S(1)} %bitcast.169, s32[1024]{0:T(1024)S(1)} %get-tuple-element.72), kind=kCustom, calls=%fused_computation.12 | custom fusion | bytes 6291648 | tf_op jit(solution)/shard_map/jit(_take)/gather | solution.py:106
  92.4 10.8 %fusion.4 = f32[48,128,256]{2,1,0:T(8,128)} fusion(bf16[48,256,256]{2,1,0:T(8,128)(2,1)} %gather_fusion.1, pred[48]{0:T(512)(128)(4,1)S(1)} %get-tuple-element.77, bf16[48,128,256]{2,1,0:T(8,128)(2,1)} %gather_fusion.2, pred[48]{0:T(512)(128)(4,1)S(1)} %get-tuple-element.68, f32[48,128,128]{2,1,0:T(8,128)} %get-tuple-element.51, f32[48]{0:T(128)S(1)} %get-tuple-element.67), kind=kOutput, calls=%fused_computation.24 | convolution fusion | flops 1215823872 | bytes 18874656 | tf_op jit(solution)/shard_map/pbd,pcd->pbc/dot_general | solution.py:115
  103.2 8.3 %fusion = f32[6,128,256]{2,0,1:T(8,128)S(1)} fusion(f32[48,128,256]{2,1,0:T(8,128)} %fusion.4, s32[48]{0:T(128)S(1)} %copy-done.7), kind=kOutput, calls=%fused_computation.14 | convolution fusion | flops 113246496 | bytes 7078080 | tf_op jit(solution)/shard_map/jp,pbc->jbc/dot_general | solution.py:131
  111.6 0.4 fusion.82
  112.0 0.9 fusion.57
  112.9 10.8 %fusion.10 = (f32[48,128,128]{2,1,0:T(8,128)S(1)}, f32[48,128,128]{2,1,0:T(8,128)}, f32[48,128,128]{2,1,0:T(8,128)}) fusion(f32[3,48,128,128]{3,2,1,0:T(8,128)} %get-tuple-element.50, bf16[48,128,256]{2,1,0:T(8,128)(2,1)} %copy-done.3, bf16[48,128,256]{2,1,0:T(8,128)(2,1)} %gather_fusion.2, pred[48]{0:T(512)(128)(4,1)S(1)} %get-tuple-element.68, ...), kind=kOutput, calls=%fused_computation.32 | convolution fusion | flops 408944640 | bytes 28311984 | tf_op jit(solution)/shard_map/pad,pbd->pab/dot_general | solution.py:109
  123.8 9.7 %fusion.30 = (f32[48,128]{1,0:T(8,128)S(1)}, f32[48,128]{1,0:T(8,128)S(1)}, f32[48,128]{1,0:T(8,128)S(1)}, f32[48,128]{1,0:T(8,128)S(1)}, f32[48,128]{1,0:T(8,12...) fusion(f32[48,128,128]{2,1,0:T(8,128)} %get-tuple-element.45, ...), kind=kLoop, calls=%fused_computation.49 | loop fusion | flops 18763776 | bytes 19316736 | tf_op jit(solution)/shard_map/reduce_sum | solution.py:127
  133.8 4.9 %collective-permute-start.12 = (f32[9,128]{1,0:T(8,128)S(1)}, f32[9,128]{1,0:T(8,128)S(1)}, u32[]{:S(2)}, u32[]{:S(2)}) collective-permute-start(f32[9,128]{1,0:T(8,128)S(1)} %get-tuple-element.52), channel_id=1, source_target_pairs={{0,28},{4,0},{8,4},{12,8},{16,12},{20,16},{24,20},{28,24},{1,29},{... | collective-permute-start | bytes 13832 | tf_op jit(solution)/shard_map/ppermute | solution.py:17
  138.7 3.3 %collective-permute-start.14 = (f32[9,128]{1,0:T(8,128)S(1)}, f32[9,128]{1,0:T(8,128)S(1)}, u32[]{:S(2)}, u32[]{:S(2)}) collective-permute-start(f32[9,128]{1,0:T(8,128)S(1)} %get-tuple-element.54), channel_id=1, source_target_pairs={{0,24},{4,28},{8,0},{12,4},{16,8},{20,12},{24,16},{28,20},{1,25},{... | collective-permute-start | bytes 13832 | tf_op jit(solution)/shard_map/ppermute | solution.py:17
  142.4 0.5 collective-permute-done.15
  143.0 3.9 %collective-permute-start.10 = (f32[128,256]{1,0:T(8,128)S(1)}, f32[128,256]{1,0:T(8,128)S(1)}, u32[]{:S(2)}, u32[]{:S(2)}) collective-permute-start(f32[128,256]{1,0:T(8,128)S(1)} %bitcast.182), channel_id=1, source_target_pairs={{0,24},{4,28},{8,0},{12,4},{16,8},{20,12},{24,16},{28,20},{1,25},{... | collective-permute-start | bytes 393224 | tf_op jit(solution)/shard_map/ppermute | solution.py:17
  147.4 3.1 %collective-permute-start.8 = (f32[128,256]{1,0:T(8,128)S(1)}, f32[128,256]{1,0:T(8,128)S(1)}, u32[]{:S(2)}, u32[]{:S(2)}) collective-permute-start(f32[128,256]{1,0:T(8,128)S(1)} %bitcast.180), channel_id=1, source_target_pairs={{0,28},{4,0},{8,4},{12,8},{16,12},{20,16},{24,20},{28,24},{1,29},{... | collective-permute-start | bytes 393224 | tf_op jit(solution)/shard_map/ppermute | solution.py:17
  150.9 0.4 fusion.48
  151.3 0.4 fusion.46
  151.7 1.2 collective-permute-done.11
  153.0 0.4 fusion.44
  153.3 0.6 collective-permute-done.8
  154.0 0.4 fusion.39
  154.4 16.4 %all-reduce.4 = (bf16[256,256]{1,0:T(8,128)(2,1)}, f32[9,256]{1,0:T(8,128)S(1)}) all-reduce(f32[256,256]{1,0:T(8,128)S(1)} %fusion.39, f32[9,256]{1,0:T(8,128)S(1)} %fusion.42), channel_id=1, replica_groups=mesh['dom'=8,'rep'=4] {'rep'}, use_global_device_ids=true, to_apply=%region_3.7 | all-reduce | flops 67840 | bytes 411648 | tf_op jit(solution)/shard_map/psum | solution.py:159
  170.8 0.6 slice.155
  171.4 0.6 slice.156
  172.0 3.0 %reduce-scatter.2.cloned.1.call-done = f32[32,64]{1,0:T(8,128)} async-done(((f32[256,64]{1,0:T(8,128)}), f32[32,64]{1,0:T(8,128)}) %reduce-scatter.2.cloned.1.call-update) | async-done | bytes 8208 | tf_op jit(solution)/shard_map/reduce_scatter | solution.py:105
  (133 shorter events, 4.3 us)
Async XLA Ops:
  7.2 20.9 %copy-start = (bf16[8,256,256]{2,1,0:T(8,128)(2,1)S(1)}, bf16[8,256,256]{2,1,0:T(8,128)(2,1)}, u32[]{:S(2)}) copy-start(bf16[8,256,256]{2,1,0:T(8,128)(2,1)} %param.19) | copy-start | bytes 3145732
  7.2 18.4 %copy-start.6 = (s32[4,128]{1,0:T(4,128)S(1)}, s32[4,128]{1,0:T(4,128)}, u32[]{:S(2)}) copy-start(s32[4,128]{1,0:T(4,128)} %param.23) | copy-start | bytes 6148
  7.2 20.3 %copy-start.1 = (bf16[256,256]{1,0:T(8,128)(2,1)S(1)}, bf16[256,256]{1,0:T(8,128)(2,1)}, u32[]{:S(2)}) copy-start(bf16[256,256]{1,0:T(8,128)(2,1)} %param.17) | copy-start | bytes 393220
  7.2 20.7 %copy-start.5 = (f32[3,256]{1,0:T(4,128)S(1)}, f32[3,256]{1,0:T(4,128)}, u32[]{:S(2)}) copy-start(f32[3,256]{1,0:T(4,128)} %param.18) | copy-start | bytes 9220
  7.2 18.2 %copy-start.10 = (s32[48]{0:T(128)S(1)}, s32[48]{0:T(128)}, u32[]{:S(2)}) copy-start(s32[48]{0:T(128)} %param.26) | copy-start | bytes 580
  7.2 18.2 %copy-start.7 = (s32[48]{0:T(128)S(1)}, s32[48]{0:T(128)}, u32[]{:S(2)}) copy-start(s32[48]{0:T(128)} %param.25) | copy-start | bytes 580
  7.2 18.3 %copy-start.9 = (s32[48]{0:T(128)S(1)}, s32[48]{0:T(128)}, u32[]{:S(2)}) copy-start(s32[48]{0:T(128)} %param.24) | copy-start | bytes 580
  7.2 20.3 %copy-start.12 = (f32[8]{0:T(128)S(1)}, f32[8]{0:T(128)}, u32[]{:S(2)}) copy-start(f32[8]{0:T(128)} %param.22) | copy-start | bytes 100
  7.3 20.4 %copy-start.8 = (s32[3,48]{1,0:T(4,128)S(1)}, s32[3,48]{1,0:T(4,128)}, u32[]{:S(2)}) copy-start(s32[3,48]{1,0:T(4,128)} %param.27) | copy-start | bytes 1732
  7.3 167.8 %reduce-scatter.2.cloned.1.call-start = ((), (), s32[]{:S(2)}) async-start(), calls=%async_computation.1 | async-start | bytes 147456 | tf_op jit(solution)/shard_map/reduce_scatter | solution.py:105
  9.9 46.5 %collective-permute-start.7 = (bf16[128,256]{1,0:T(8,128)(2,1)S(1)}, bf16[128,256]{1,0:T(8,128)(2,1)S(1)}, u32[]{:S(2)}, u32[]{:S(2)}) collective-permute-start(bf16[128,256]{1,0:T(8,128)(2,1)S(1)} %broadcast_select_fusion.9), channel_id=1, source_target_pairs={{0,24},{4,28},{8,0},{12,4},{16,8},{20,12},{24,16},{28,20},{1,25},{... | collective-permute-start | bytes 196616 | tf_op jit(solution)/shard_map/ppermute | solution.py:17
  15.9 40.5 %collective-permute-start.6 = (bf16[128,256]{1,0:T(8,128)(2,1)S(1)}, bf16[128,256]{1,0:T(8,128)(2,1)S(1)}, u32[]{:S(2)}, u32[]{:S(2)}) collective-permute-start(bf16[128,256]{1,0:T(8,128)(2,1)S(1)} %broadcast_select_fusion.10), channel_id=1, source_target_pairs={{0,8},{4,12},{8,16},{12,20},{16,24},{20,28},{24,0},{28,4},{1,9},{5... | collective-permute-start | bytes 196616 | tf_op jit(solution)/shard_map/ppermute | solution.py:17
  17.7 38.6 %collective-permute-start.5 = (bf16[128,256]{1,0:T(8,128)(2,1)S(1)}, bf16[128,256]{1,0:T(8,128)(2,1)S(1)}, u32[]{:S(2)}, u32[]{:S(2)}) collective-permute-start(bf16[128,256]{1,0:T(8,128)(2,1)S(1)} %broadcast_select_fusion.11), channel_id=1, source_target_pairs={{0,28},{4,0},{8,4},{12,8},{16,12},{20,16},{24,20},{28,24},{1,29},{... | collective-permute-start | bytes 196616 | tf_op jit(solution)/shard_map/ppermute | solution.py:17
  23.7 32.6 %collective-permute-start.4 = (bf16[128,256]{1,0:T(8,128)(2,1)S(1)}, bf16[128,256]{1,0:T(8,128)(2,1)S(1)}, u32[]{:S(2)}, u32[]{:S(2)}) collective-permute-start(bf16[128,256]{1,0:T(8,128)(2,1)S(1)} %broadcast_select_fusion.12), channel_id=1, source_target_pairs={{0,4},{4,8},{8,12},{12,16},{16,20},{20,24},{24,28},{28,0},{1,5},{5... | collective-permute-start | bytes 196616 | tf_op jit(solution)/shard_map/ppermute | solution.py:17
  25.4 7.7 %collective-permute-start = (f32[3,128]{0,1:T(8,128)S(1)}, f32[3,128]{0,1:T(8,128)S(1)}, u32[]{:S(2)}, u32[]{:S(2)}) collective-permute-start(f32[3,128]{0,1:T(8,128)S(1)} %select_bitcast_fusion.4), channel_id=1, source_target_pairs={{0,4},{4,8},{8,12},{12,16},{16,20},{20,24},{24,28},{28,0},{1,5},{5... | collective-permute-start | bytes 4616 | tf_op jit(solution)/shard_map/ppermute | solution.py:17
  33.0 5.5 %collective-permute-start.1 = (f32[3,128]{0,1:T(8,128)S(1)}, f32[3,128]{0,1:T(8,128)S(1)}, u32[]{:S(2)}, u32[]{:S(2)}) collective-permute-start(f32[3,128]{0,1:T(8,128)S(1)} %select_bitcast_fusion.3), channel_id=1, source_target_pairs={{0,28},{4,0},{8,4},{12,8},{16,12},{20,16},{24,20},{28,24},{1,29},{... | collective-permute-start | bytes 4616 | tf_op jit(solution)/shard_map/ppermute | solution.py:17
  38.5 4.9 %collective-permute-start.2 = (f32[3,128]{0,1:T(8,128)S(1)}, f32[3,128]{0,1:T(8,128)S(1)}, u32[]{:S(2)}, u32[]{:S(2)}) collective-permute-start(f32[3,128]{0,1:T(8,128)S(1)} %select_bitcast_fusion.2), channel_id=1, source_target_pairs={{0,8},{4,12},{8,16},{12,20},{16,24},{20,28},{24,0},{28,4},{1,9},{5... | collective-permute-start | bytes 4616 | tf_op jit(solution)/shard_map/ppermute | solution.py:17
  43.4 3.8 %collective-permute-start.3 = (f32[3,128]{0,1:T(8,128)S(1)}, f32[3,128]{0,1:T(8,128)S(1)}, u32[]{:S(2)}, u32[]{:S(2)}) collective-permute-start(f32[3,128]{0,1:T(8,128)S(1)} %select_bitcast_fusion.1), channel_id=1, source_target_pairs={{0,24},{4,28},{8,0},{12,4},{16,8},{20,12},{24,16},{28,20},{1,25},{... | collective-permute-start | bytes 4616 | tf_op jit(solution)/shard_map/ppermute | solution.py:17
  59.0 5.3 %copy-start.2 = (f32[48,128,128]{2,1,0:T(8,128)S(1)}, f32[48,128,128]{2,1,0:T(8,128)}, u32[]{:S(2)}) copy-start(f32[48,128,128]{2,1,0:T(8,128)} %get-tuple-element.51) | copy-start | bytes 9437188
  64.2 1.8 copy-start.3
  66.0 23.3 %copy-start.4 = (bf16[256,256]{1,0:T(8,128)(2,1)S(1)}, bf16[256,256]{1,0:T(8,128)(2,1)}, u32[]{:S(2)}) copy-start(bf16[256,256]{1,0:T(8,128)(2,1)} %param.20) | copy-start | bytes 393220
  66.0 23.3 %copy-start.11 = (f32[256]{0:T(256)S(1)}, f32[256]{0:T(256)}, u32[]{:S(2)}) copy-start(f32[256]{0:T(256)} %param.21) | copy-start | bytes 3076
  112.9 10.9 %slice-start = ((s8[9437184]{0:T(1024)(128)(4,1)}), s8[4194304]{0:T(1024)(128)(4,1)S(1)}, s32[]{:S(2)}) async-start(s8[9437184]{0:T(1024)(128)(4,1)} %bitcast.170), calls=%async_computation.2 | async-start | bytes 8388608
  112.9 10.9 %slice-start.1 = ((s8[9437184]{0:T(1024)(128)(4,1)}), s8[4194304]{0:T(1024)(128)(4,1)S(1)}, s32[]{:S(2)}) async-start(s8[9437184]{0:T(1024)(128)(4,1)} %bitcast.170), calls=%async_computation.3 | async-start | bytes 8388608
  112.9 10.8 %slice-start.2 = ((s8[9437184]{0:T(1024)(128)(4,1)}), s8[1048576]{0:T(1024)(128)(4,1)S(1)}, s32[]{:S(2)}) async-start(s8[9437184]{0:T(1024)(128)(4,1)} %bitcast.170), calls=%async_computation.4 | async-start | bytes 2097152
  133.8 16.9 %collective-permute-start.12 = (f32[9,128]{1,0:T(8,128)S(1)}, f32[9,128]{1,0:T(8,128)S(1)}, u32[]{:S(2)}, u32[]{:S(2)}) collective-permute-start(f32[9,128]{1,0:T(8,128)S(1)} %get-tuple-element.52), channel_id=1, source_target_pairs={{0,28},{4,0},{8,4},{12,8},{16,12},{20,16},{24,20},{28,24},{1,29},{... | collective-permute-start | bytes 13832 | tf_op jit(solution)/shard_map/ppermute | solution.py:17
  138.7 4.3 %collective-permute-start.15 = (f32[9,128]{1,0:T(8,128)S(1)}, f32[9,128]{1,0:T(8,128)S(1)}, u32[]{:S(2)}, u32[]{:S(2)}) collective-permute-start(f32[9,128]{1,0:T(8,128)S(1)} %get-tuple-element.53), channel_id=1, source_target_pairs={{0,8},{4,12},{8,16},{12,20},{16,24},{20,28},{24,0},{28,4},{1,9},{5... | collective-permute-start | bytes 13832 | tf_op jit(solution)/shard_map/ppermute | solution.py:17
  138.7 8.4 %collective-permute-start.14 = (f32[9,128]{1,0:T(8,128)S(1)}, f32[9,128]{1,0:T(8,128)S(1)}, u32[]{:S(2)}, u32[]{:S(2)}) collective-permute-start(f32[9,128]{1,0:T(8,128)S(1)} %get-tuple-element.54), channel_id=1, source_target_pairs={{0,24},{4,28},{8,0},{12,4},{16,8},{20,12},{24,16},{28,20},{1,25},{... | collective-permute-start | bytes 13832 | tf_op jit(solution)/shard_map/ppermute | solution.py:17
  141.9 5.4 %collective-permute-start.13 = (f32[9,128]{1,0:T(8,128)S(1)}, f32[9,128]{1,0:T(8,128)S(1)}, u32[]{:S(2)}, u32[]{:S(2)}) collective-permute-start(f32[9,128]{1,0:T(8,128)S(1)} %get-tuple-element.55), channel_id=1, source_target_pairs={{0,4},{4,8},{8,12},{12,16},{16,20},{20,24},{24,28},{28,0},{1,5},{5... | collective-permute-start | bytes 13832 | tf_op jit(solution)/shard_map/ppermute | solution.py:17
  142.4 8.6 %collective-permute-start.9 = (f32[128,256]{1,0:T(8,128)S(1)}, f32[128,256]{1,0:T(8,128)S(1)}, u32[]{:S(2)}, u32[]{:S(2)}) collective-permute-start(f32[128,256]{1,0:T(8,128)S(1)} %bitcast.183), channel_id=1, source_target_pairs={{0,4},{4,8},{8,12},{12,16},{16,20},{20,24},{24,28},{28,0},{1,5},{5... | collective-permute-start | bytes 393224 | tf_op jit(solution)/shard_map/ppermute | solution.py:17
  143.0 8.4 %collective-permute-start.10 = (f32[128,256]{1,0:T(8,128)S(1)}, f32[128,256]{1,0:T(8,128)S(1)}, u32[]{:S(2)}, u32[]{:S(2)}) collective-permute-start(f32[128,256]{1,0:T(8,128)S(1)} %bitcast.182), channel_id=1, source_target_pairs={{0,24},{4,28},{8,0},{12,4},{16,8},{20,12},{24,16},{28,20},{1,25},{... | collective-permute-start | bytes 393224 | tf_op jit(solution)/shard_map/ppermute | solution.py:17
  147.1 5.9 %collective-permute-start.11 = (f32[128,256]{1,0:T(8,128)S(1)}, f32[128,256]{1,0:T(8,128)S(1)}, u32[]{:S(2)}, u32[]{:S(2)}) collective-permute-start(f32[128,256]{1,0:T(8,128)S(1)} %bitcast.181), channel_id=1, source_target_pairs={{0,8},{4,12},{8,16},{12,20},{16,24},{20,28},{24,0},{28,4},{1,9},{5... | collective-permute-start | bytes 393224 | tf_op jit(solution)/shard_map/ppermute | solution.py:17
  147.4 6.6 %collective-permute-start.8 = (f32[128,256]{1,0:T(8,128)S(1)}, f32[128,256]{1,0:T(8,128)S(1)}, u32[]{:S(2)}, u32[]{:S(2)}) collective-permute-start(f32[128,256]{1,0:T(8,128)S(1)} %bitcast.180), channel_id=1, source_target_pairs={{0,28},{4,0},{8,4},{12,8},{16,12},{20,16},{24,20},{28,24},{1,29},{... | collective-permute-start | bytes 393224 | tf_op jit(solution)/shard_map/ppermute | solution.py:17
Sparse Core Ops, SparseCore 0:
  113.0 61.9 reduce-scatter.1
where the time goes:
time: 185 us; the launch traced here: 182 us
  matrix products  45.9 us (25%)
  blocking collectives  34.1 us (18%)
  starting transfers between devices  28.2 us (15%)
  local copies, waits for them, and re-layouts  24.5 us (13%)
  other arithmetic  19.1 us (10%)
  waiting for transfers between devices  15.1 us (8%)
  between operations  14.9 us (8%)
    ppermute x16, starting transfers between devices, from_behind(): lax.ppermute(array, axis, [(i, (i + by) % count) for i in range(count)])  28.2 us
    psum x1, blocking collectives, on_device(): message = lax.psum(message_portion, 'rep')  17.6 us
    psum x1, blocking collectives, on_device(): totals = lax.psum((own_grad, self_side), 'rep')  16.4 us
    ppermute x16, waiting for transfers between devices, from_behind(): lax.ppermute(array, axis, [(i, (i + by) % count) for i in range(count)])  12.1 us
    dot_general x1, matrix products, on_device(): jnp.einsum('pad,pbd->pab', adjoint_tiles, mapped, preferred_element_type=...  10.8 us
    dot_general x1, matrix products, on_device(): jnp.einsum('pbd,pcd->pbc', mapped_grad, chosen, preferred_element_type=jn...  10.8 us
    reduce_sum x1, other arithmetic, on_device(): home_atom_side.append(-0.5 * jnp.sum(product, axis=2))  9.67 us
    dot_general x1, matrix products, on_device(): jnp.einsum('jp,pbc->jbc', partner_table, feature_grad, precision=highest_...  8.28 us
  transfers between devices with their start and end apart: 17, of which 7 were waited for; matrix products, arithmetic and copies ran while one was open for 27% of the time, Pallas kernels for 0%

commit v1 on v0

v1 whole, which is shorter than its diff:
```python
import functools

import jax
import jax.numpy as jnp
from jax import lax
from jax.experimental import pallas as pl
from jax.experimental.pallas import tpu as pltpu
from jax.sharding import PartitionSpec as P

TILE = 128
OFFSETS = (1, -1, 2, -2)
CELL = 2.0
GROUP = 4
F32 = jnp.float32
BF16 = jnp.bfloat16
MESH = pl.DeviceIdType.MESH
VMEM = pl.BlockSpec(memory_space=pltpu.VMEM)
SMEM = pl.BlockSpec(memory_space=pltpu.SMEM)


def nt(a, b):
    return lax.dot_general(a, b, (((1,), (1,)), ((), ())), preferred_element_type=F32)


def tn(a, b):
    return lax.dot_general(a, b, (((0,), (0,)), ((), ())), preferred_element_type=F32)


def mm(a, b):
    return jnp.dot(a, b, preferred_element_type=F32)


def split3(x):
    hi = x.astype(BF16)
    rest = x - hi.astype(F32)
    mid = rest.astype(BF16)
    low = (rest - mid.astype(F32)).astype(BF16)
    return hi, mid, low


def halo_kernel(n_dom, feat, pos, rows, radial, mapped, tiles, sendf, sendp, recvf, recvp,
                sf, sp, rf, rp):
    d = lax.axis_index("dom")
    r = lax.axis_index("rep")
    barrier = pltpu.get_barrier_semaphore()
    for o in OFFSETS:
        pl.semaphore_signal(barrier, inc=1, device_id={"dom": lax.rem(d + o + n_dom, n_dom), "rep": r},
                            device_id_type=MESH)
    atoms = feat.shape[0]
    iota = lax.broadcasted_iota(jnp.int32, (atoms, TILE), 0)
    for t in range(4):
        hot = (iota == rows[t:t + 1, :]).astype(F32)
        sendf[t] = tn(hot.astype(BF16), feat[...]).astype(BF16)
        sendp[t] = jnp.dot(pos[...], hot, precision=lax.Precision.HIGHEST, preferred_element_type=F32)
    pl.semaphore_wait(barrier, 4)
    copies = []
    for t, o in enumerate(OFFSETS):
        to = {"dom": lax.rem(d + o + n_dom, n_dom), "rep": r}
        cf = pltpu.make_async_remote_copy(sendf.at[t], recvf.at[t], sf.at[t], rf.at[t],
                                          device_id=to, device_id_type=MESH)
        cp = pltpu.make_async_remote_copy(sendp.at[t], recvp.at[t], sp.at[t], rp.at[t],
                                          device_id=to, device_id_type=MESH)
        cf.start()
        cp.start()
        copies.append((cf, cp))
    own = atoms // TILE
    for j in range(own):
        tiles[j] = pos[:, j * TILE:(j + 1) * TILE]

    def local(k, _):
        res = mm(feat[...], radial[k]).astype(BF16)
        for j in range(own):
            mapped[j, k] = res[j * TILE:(j + 1) * TILE]
        return 0

    lax.fori_loop(0, radial.shape[0], local, 0)
    for h in range(2):
        for t in (2 * h, 2 * h + 1):
            copies[t][0].wait_recv()
            copies[t][1].wait_recv()
            tiles[own + t] = recvp[t]

        def far(k, _):
            both = jnp.concatenate([recvf[2 * h], recvf[2 * h + 1]], axis=0)
            res = mm(both, radial[k]).astype(BF16)
            mapped[own + 2 * h, k] = res[:TILE]
            mapped[own + 2 * h + 1, k] = res[TILE:]
            return 0

        lax.fori_loop(0, radial.shape[0], far, 0)
    for cf, cp in copies:
        cf.wait_send()
        cp.wait_send()


def forward_kernel(decay, home, other, kind, image, tiles, mapped, out, near, acc):
    for i in range(2):
        for c in range(3):
            near[i, c] = jnp.transpose(jnp.broadcast_to(tiles[i][c:c + 1, :], (TILE, TILE)))
    acc[...] = jnp.zeros_like(acc)

    def body(g, _):
        found = []
        for u in range(GROUP):
            p = g * GROUP + u
            h, o, k = home[p], other[p], kind[p]
            rate = decay[k]
            row = tiles[o]
            d2 = None
            for c in range(3):
                sep = (row[c:c + 1, :] + image[c, p].astype(F32) * CELL) - near[h, c]
                d2 = sep * sep if d2 is None else d2 + sep * sep
            kern = jnp.exp(d2 * (-rate)).astype(BF16)
            found.append((h, mm(kern, mapped[o, k])))
        for h, m in found:
            acc[h] += m
        return 0

    lax.fori_loop(0, home.shape[0] // GROUP, body, 0)
    share = out.shape[1]
    per = TILE // share
    for i in range(2):
        for q in range(per):
            out[i * per + q] = acc[i, q * share:(q + 1) * share, :].astype(BF16)


def atom_kernel(n_rep, msg, mixing, readout, packed, slope, adjoint, recv, pk, sl, s1, r1, s2, r2, s3, r3):
    d = lax.axis_index("dom")
    r = lax.axis_index("rep")
    barrier = pltpu.get_barrier_semaphore()
    peers = [lax.rem(r + i, n_rep) for i in range(1, n_rep)]
    for q in peers:
        pl.semaphore_signal(barrier, inc=1, device_id={"dom": d, "rep": q}, device_id_type=MESH)
    pl.semaphore_wait(barrier, n_rep - 1)

    def push(src, dst, ss, rs, q):
        copy = pltpu.make_async_remote_copy(src, dst, ss, rs, device_id={"dom": d, "rep": q},
                                            device_id_type=MESH)
        copy.start()
        return copy

    def take(dst, ss, rs, q):
        pltpu.make_async_remote_copy(dst, dst, ss, rs, device_id={"dom": d, "rep": q},
                                     device_id_type=MESH).wait_recv()

    sent = [push(msg.at[q], recv.at[r], s1.at[i], r1.at[r], q) for i, q in enumerate(peers)]
    total = msg[r].astype(F32)
    for i, q in enumerate(peers):
        take(recv.at[q], s1.at[i], r1.at[q], q)
        total = total + recv[q].astype(F32)
    low = total.astype(BF16)
    pk[r] = low
    sent += [push(pk.at[r], pk.at[r], s2.at[i], r2.at[r], q) for i, q in enumerate(peers)]
    mixed = mm(low, mixing[...])
    sig = jax.nn.sigmoid(mixed)
    sl[r] = (readout[...] * sig * (1.0 + mixed * (1.0 - sig))).astype(BF16)
    sent += [push(sl.at[r], sl.at[r], s3.at[i], r3.at[r], q) for i, q in enumerate(peers)]
    for i, q in enumerate(peers):
        take(sl.at[q], s3.at[i], r3.at[q], q)
    full = sl[...].reshape(-1, mixing.shape[0])
    slope[...] = full
    adj = nt(full, mixing[...]).astype(BF16)
    for j in range(adjoint.shape[0]):
        adjoint[j] = adj[j * TILE:(j + 1) * TILE]
    for i, q in enumerate(peers):
        take(pk.at[q], s2.at[i], r2.at[q], q)
    packed[...] = pk[...].reshape(-1, mixing.shape[0])
    for copy in sent:
        copy.wait_send()


def backward_kernel(n_rep, decay, home, other, kind, image, tiles, mapped, adjoint, radial, packed, slope,
                    gfeat, side, mix, far, moments, first, second, acc):
    n_ext = tiles.shape[0]
    for j in range(n_ext):
        pos = tiles[j]
        x, y, z = pos[0:1, :], pos[1:2, :], pos[2:3, :]
        for c in range(3):
            far[j, c] = jnp.transpose(jnp.broadcast_to(pos[c:c + 1, :], (TILE, TILE)))
        zero = jnp.zeros((2, TILE), F32)
        one_rows = jnp.concatenate([x, y, z, x, x, y, zero], axis=0)
        two_rows = jnp.concatenate([x, y, z, y, z, z, zero], axis=0)
        first[j] = one_rows
        second[j] = two_rows
        stack = jnp.concatenate([one_rows * two_rows, one_rows, two_rows], axis=0)
        parts = [v.astype(F32) for v in split3(stack)]
        moments[j] = jnp.concatenate(
            [parts[0], jnp.ones((8, TILE), F32), parts[1], parts[2]], axis=0).astype(BF16)
    acc[...] = jnp.zeros_like(acc)
    side[...] = jnp.zeros_like(side)
    sub = lax.broadcasted_iota(jnp.int32, (8, TILE), 0)

    def rows_of(a, b):
        return ((sub == a[0]) | (sub == a[1]) | (sub == a[2])), ((sub == b[0]) | (sub == b[1]))

    is_x1, is_y1 = rows_of((0, 3, 4), (1, 5))
    is_x2, is_y2 = (sub == 0), ((sub == 1) | (sub == 3))

    def fold(res):
        quad = res[0:8] + res[32:40] + res[56:64]
        lin1 = res[8:16] + res[40:48] + res[64:72]
        lin2 = res[16:24] + res[48:56] + res[72:80]
        return quad, lin1, lin2, res[24:32]

    def combine(res, a, b):
        quad, lin1, lin2, one = fold(res)
        force = lin1 - a * one
        virial = -0.5 * (quad - a * lin2 - b * lin1 + a * b * one)
        return jnp.concatenate([force, virial], axis=0)

    def body(g, _):
        found = []
        for u in range(GROUP):
            p = g * GROUP + u
            h, o, k = home[p], other[p], kind[p]
            rate = decay[k]
            shift = [image[c, p].astype(F32) * CELL for c in range(3)]
            row = tiles[h]
            d2 = None
            for c in range(3):
                sep = far[o, c] - (row[c:c + 1, :] - shift[c])
                d2 = sep * sep if d2 is None else d2 + sep * sep
            kern = jnp.exp(d2 * (-rate))
            adj = adjoint[h]
            weight = (-2.0 * rate) * kern * nt(mapped[o, k], adj)
            back = mm(kern.astype(BF16), adj).astype(BF16)
            part = nt(back, radial[k])
            hi = weight.astype(BF16)
            lo = (weight - hi.astype(F32)).astype(BF16)
            near_res = mm(moments[o], hi) + mm(moments[o], lo)
            far_res = nt(moments[h], hi) + nt(moments[h], lo)
            s1 = jnp.where(is_x1, shift[0], jnp.where(is_y1, shift[1], shift[2]))
            s2 = jnp.where(is_x2, shift[0], jnp.where(is_y2, shift[1], shift[2]))
            near_side = combine(near_res, first[h] - s1, second[h] - s2)
            far_side = combine(far_res, first[o] + s1, second[o] + s2)
            found.append((h, o, part, near_side, far_side))
        for h, o, part, near_side, far_side in found:
            acc[o] += part
            side[h] += near_side
            side[o] += far_side
        return 0

    lax.fori_loop(0, home.shape[0] // GROUP, body, 0)
    for j in range(n_ext):
        for half in range(2):
            gfeat[j, half] = acc[j, :, half * TILE:(half + 1) * TILE].astype(BF16)
    r = lax.axis_index("rep")
    channels = slope.shape[1]
    share = channels // n_rep
    pick = (lax.broadcasted_iota(jnp.int32, (channels, share), 0)
            == lax.broadcasted_iota(jnp.int32, (channels, share), 1) + r * share).astype(BF16)
    cols = mm(slope[...], pick).astype(BF16)
    res = tn(packed[...], cols)
    mix[...] = res.reshape(mix.shape)


TILE_CORE = (0, 1, 0, 0, 1, 1)
TILE_SLOT = (0, 0, 1, 2, 1, 2)


def return_kernel(n_dom, n_rep, gfeat, side, mix, rows, out_feat, out_force, out_virial, out_mix,
                  rf, rs, rm, part, pside, qside,
                  sem_sf, sem_rf, sem_ss, sem_rs, sem_sm, sem_rm, sem_sp, sem_rp, sem_sq, sem_rq):
    d = lax.axis_index("dom")
    r = lax.axis_index("rep")
    y = lax.div(r, 2)
    c = lax.rem(r, 2)

    def dom_at(o):
        return lax.rem(d + o + n_dom, n_dom)

    barrier = pltpu.get_barrier_semaphore()

    def hello(dom, rep):
        pl.semaphore_signal(barrier, inc=1, device_id={"dom": dom, "rep": rep}, device_id_type=MESH)

    mine = [(c + 1), -(c + 1)]
    peers = [lax.rem(r + i, n_rep) for i in range(1, n_rep)]
    for o in mine:
        for q in range(n_rep):
            hello(dom_at(o), q)
    for q in peers:
        hello(d, q)

    def greet(i, _):
        hello(lax.rem(d + i, n_dom), r)
        return 0

    lax.fori_loop(1, n_dom, greet, 0)
    pl.semaphore_wait(barrier, 2 * n_rep + n_rep - 1 + n_dom - 1)

    sends = []
    for j in (2, 3, 4, 5, 0, 1):
        for half in range(2):
            to = half * 2 + TILE_CORE[j]
            dest = {"dom": d if j < 2 else dom_at(-OFFSETS[j - 2]), "rep": to}
            slot = TILE_SLOT[j]
            cf = pltpu.make_async_remote_copy(gfeat.at[j, half], rf.at[slot, r], sem_sf.at[j, half],
                                              sem_rf.at[slot, r], device_id=dest, device_id_type=MESH)
            cs = pltpu.make_async_remote_copy(side.at[j], rs.at[slot, r], sem_ss.at[j, half],
                                              sem_rs.at[slot, r], device_id=dest, device_id_type=MESH)
            sends.append((j, to, cf, cs))
            if j < 2:
                @pl.when(r != to)
                def _():
                    cf.start()
                    cs.start()
            else:
                cf.start()
                cs.start()

    def mix_copy(i):
        to = lax.rem(d + i, n_dom)
        return pltpu.make_async_remote_copy(mix.at[to], rm.at[d], sem_sm.at[i], sem_rm.at[d],
                                            device_id={"dom": to, "rep": r}, device_id_type=MESH)

    def mix_start(i, _):
        mix_copy(i).start()
        return 0

    lax.fori_loop(1, n_dom, mix_start, 0)

    def take(dst, ss, rsem):
        pltpu.make_async_remote_copy(dst, dst, ss, rsem, device_id={"dom": d, "rep": peers[0]},
                                     device_id_type=MESH).wait_recv()

    feat_self = gfeat[c, y].astype(F32)
    side_self = side[c]
    for q in peers:
        take(rf.at[0, q], sem_sf.at[0, 0], sem_rf.at[0, q])
        take(rs.at[0, q], sem_ss.at[0, 0], sem_rs.at[0, q])
        feat_self = feat_self + rf[0, q].astype(F32)
        side_self = side_self + rs[0, q]
    is_low = c == 0
    zero = jnp.zeros_like(feat_self)
    total = jnp.concatenate([jnp.where(is_low, feat_self, zero), jnp.where(is_low, zero, feat_self)], axis=0)
    zside = jnp.zeros_like(side_self)
    total_side = jnp.concatenate([jnp.where(is_low, side_self, zside), jnp.where(is_low, zside, side_self)],
                                 axis=1)
    atoms = out_feat.shape[0]
    iota = lax.broadcasted_iota(jnp.int32, (atoms, TILE), 0)
    for q in range(2):
        hot = (iota == rows[pl.ds(2 * c + q, 1), :]).astype(F32).astype(BF16)
        slot = 1 + q
        got = None
        for s in range(n_rep):
            take(rf.at[slot, s], sem_sf.at[0, 0], sem_rf.at[slot, s])
            take(rs.at[slot, s], sem_ss.at[0, 0], sem_rs.at[slot, s])
            total = total + mm(hot, rf[slot, s])
            got = rs[slot, s] if got is None else got + rs[slot, s]
        for v in split3(got):
            total_side = total_side + nt(v, hot)
    part[r] = total.astype(BF16)
    pside[...] = total_side
    phase = []
    for i, q in enumerate(peers):
        cp = pltpu.make_async_remote_copy(part.at[r], part.at[r], sem_sp.at[i], sem_rp.at[r],
                                          device_id={"dom": d, "rep": q}, device_id_type=MESH)
        cp.start()
        phase.append(cp)
    cq = pltpu.make_async_remote_copy(pside, qside, sem_sq, sem_rq,
                                      device_id={"dom": d, "rep": r + 1 - 2 * c}, device_id_type=MESH)
    cq.start()

    def mix_add(i, value):
        frm = lax.rem(d + i, n_dom)
        take(rm.at[frm], sem_sm.at[0], sem_rm.at[frm])
        return value + rm[frm]

    out_mix[...] = lax.fori_loop(1, n_dom, mix_add, mix[d])
    cq.wait_recv()
    final = total_side + qside[...]
    out_force[...] = final[0:3]
    out_virial[...] = final[8:14]
    for q in peers:
        take(part.at[q], sem_sp.at[0], sem_rp.at[q])
    for half in range(2):
        out_feat[:, half * TILE:(half + 1) * TILE] = (
            part[2 * half].astype(F32) + part[2 * half + 1].astype(F32)).astype(BF16)
    for j, to, cf, cs in sends:
        if j < 2:
            @pl.when(r != to)
            def _():
                cf.wait_send()
                cs.wait_send()
        else:
            cf.wait_send()
            cs.wait_send()

    def mix_done(i, _):
        mix_copy(i).wait_send()
        return 0

    lax.fori_loop(1, n_dom, mix_done, 0)
    for cp in phase:
        cp.wait_send()
    cq.wait_send()


def on_device(n_dom, n_rep, features, positions, radial, mixing, readout, decay, send_rows, pair_home,
              pair_other, pair_kind, pair_image):
    atoms, channels = features.shape
    own = atoms // TILE
    n_ext = own + len(OFFSETS)
    kinds = radial.shape[0]
    dma = pltpu.SemaphoreType.DMA
    share = atoms // n_rep

    def params(cid=None):
        if cid is None:
            return pltpu.CompilerParams(vmem_limit_bytes=40 << 20)
        return pltpu.CompilerParams(collective_id=cid, has_side_effects=True, vmem_limit_bytes=40 << 20)

    def shape(dims, dtype):
        return jax.ShapeDtypeStruct(dims, dtype)

    mapped, tiles = pl.pallas_call(
        functools.partial(halo_kernel, n_dom),
        out_shape=(shape((n_ext, kinds, TILE, channels), BF16), shape((n_ext, 3, TILE), F32)),
        in_specs=[VMEM] * 4,
        out_specs=(VMEM, VMEM),
        scratch_shapes=[
            pltpu.VMEM((4, TILE, channels), BF16), pltpu.VMEM((4, 3, TILE), F32),
            pltpu.VMEM((4, TILE, channels), BF16), pltpu.VMEM((4, 3, TILE), F32),
            dma((4,)), dma((4,)), dma((4,)), dma((4,)),
        ],
        compiler_params=params(0),
        name="halo",
    )(features, positions, send_rows, radial)

    message = pl.pallas_call(
        forward_kernel,
        out_shape=shape((n_rep, share, channels), BF16),
        in_specs=[SMEM] * 5 + [VMEM] * 2,
        out_specs=VMEM,
        scratch_shapes=[pltpu.VMEM((2, 3, TILE, TILE), F32), pltpu.VMEM((own, TILE, channels), F32)],
        compiler_params=params(),
        name="forward_pairs",
    )(decay, pair_home, pair_other, pair_kind, pair_image, tiles, mapped)

    packed, slope, adjoint = pl.pallas_call(
        functools.partial(atom_kernel, n_rep),
        out_shape=(shape((atoms, channels), BF16), shape((atoms, channels), BF16),
                   shape((own, TILE, channels), BF16)),
        in_specs=[VMEM] * 3,
        out_specs=(VMEM,) * 3,
        scratch_shapes=[pltpu.VMEM((n_rep, share, channels), BF16)] * 3
        + [dma((n_rep,)) for _ in range(6)],
        compiler_params=params(1),
        name="atoms",
    )(message, mixing, readout.reshape(1, channels))

    gfeat, side, mix = pl.pallas_call(
        functools.partial(backward_kernel, n_rep),
        out_shape=(shape((n_ext, 2, TILE, channels // 2), BF16), shape((n_ext, 16, TILE), F32),
                   shape((n_dom, channels // n_dom, channels // n_rep), F32)),
        in_specs=[SMEM] * 5 + [VMEM] * 6,
        out_specs=(VMEM,) * 3,
        scratch_shapes=[
            pltpu.VMEM((n_ext, 3, TILE, TILE), F32), pltpu.VMEM((n_ext, 80, TILE), BF16),
            pltpu.VMEM((n_ext, 8, TILE), F32), pltpu.VMEM((n_ext, 8, TILE), F32),
            pltpu.VMEM((n_ext, TILE, channels), F32),
        ],
        compiler_params=params(),
        name="backward_pairs",
    )(decay, pair_home, pair_other, pair_kind, pair_image, tiles, mapped, adjoint, radial, packed, slope)

    mix_rows, mix_cols = channels // n_dom, channels // n_rep
    return pl.pallas_call(
        functools.partial(return_kernel, n_dom, n_rep),
        out_shape=(shape((atoms, channels), BF16), shape((3, atoms), F32), shape((6, atoms), F32),
                   shape((mix_rows, mix_cols), F32)),
        in_specs=[VMEM] * 4,
        out_specs=(VMEM,) * 4,
        scratch_shapes=[
            pltpu.VMEM((3, n_rep, TILE, channels // 2), BF16), pltpu.VMEM((3, n_rep, 16, TILE), F32),
            pltpu.VMEM((n_dom, mix_rows, mix_cols), F32), pltpu.VMEM((n_rep, atoms, channels // 2), BF16),
            pltpu.VMEM((16, atoms), F32), pltpu.VMEM((16, atoms), F32),
            dma((n_ext, 2)), dma((3, n_rep)), dma((n_ext, 2)), dma((3, n_rep)),
            dma((n_dom,)), dma((n_dom,)), dma((n_rep,)), dma((n_rep,)), dma, dma,
        ],
        compiler_params=params(2),
        name="return_gradients",
    )(gfeat, side, mix, send_rows)


def solution(mesh):
    in_specs = (
        P("dom", None),
        P(None, "dom"),
        P(),
        P(),
        P(),
        P(),
        P(None, "dom"),
        P(("dom", "rep")),
        P(("dom", "rep")),
        P(("dom", "rep")),
        P(None, ("dom", "rep")),
    )
    out_specs = (P("dom", None), P(None, "dom"), P(None, "dom"), P("dom", "rep"))
    body = functools.partial(on_device, mesh.shape["dom"], mesh.shape["rep"])
    return jax.shard_map(body, mesh=mesh, in_specs=in_specs, out_specs=out_specs, check_vma=False)
```

time: 185 us -> 67.4 us (0.36); the launches traced: 182 us -> 67.1 us
  Pallas kernels: 0 us -> 57.1 us
  matrix products: 45.9 us -> 0 us
  blocking collectives: 34.1 us -> 0 us
  starting transfers between devices: 28.2 us -> 0 us
  other arithmetic: 19.1 us -> 0 us
  local copies, waits for them, and re-layouts: 24.5 us -> 9.26 us
  waiting for transfers between devices: 15.1 us -> 0 us
  between operations: 14.9 us -> 0.75 us
    pallas_call x0 -> x5, Pallas kernels: none -> 57.1 us  [the longest x1 16.9 us: on_device(): pl.pallas_call(functools.partial(return_kernel, n_dom, n_rep), out_shape=...]
    dot_general x19 -> x0, matrix products: 45.9 us -> none  [the longest x1 10.8 us: on_device(): jnp.einsum('pad,pbd->pab', adjoint_tiles, mapped, preferred_element_type=...]
    psum x2 -> x0, blocking collectives: 34.1 us -> none  [the longest x1 17.6 us: on_device(): message = lax.psum(message_portion, 'rep')]
    ppermute x16 -> x0, starting transfers between devices: 28.2 us -> none  [from_behind(): lax.ppermute(array, axis, [(i, (i + by) % count) for i in range(count)])]
    gather x13 -> x0, local copies, waits for them, and re-layouts: 20.7 us -> none  [the longest x4 6.71 us: on_device(): picked_feat = jnp.take(features, send_rows[section_no], axis=0)]
    ppermute x16 -> x0, waiting for transfers between devices: 12.1 us -> none  [from_behind(): lax.ppermute(array, axis, [(i, (i + by) % count) for i in range(count)])]
    reduce_sum x2 -> x0, other arithmetic: 9.75 us -> none  [the longest x1 9.67 us: on_device(): home_atom_side.append(-0.5 * jnp.sum(product, axis=2))]
    unnamed x52 -> x30, local copies, waits for them, and re-layouts: 1.73 us -> 9.26 us
  transfers between devices with their start and end apart: 17 -> 0, of which waited for: 7 -> 0; matrix products, arithmetic and copies ran while one was open for 27% -> 0% of each run, Pallas kernels for 0% -> 0%
where the time goes in v1:
time: 67.4 us; the launch traced here: 67.1 us
  Pallas kernels  57.1 us (85%)
  local copies, waits for them, and re-layouts  9.26 us (14%)
  between operations  0.75 us (1%)
    pallas_call x1, Pallas kernels, on_device(): pl.pallas_call(functools.partial(return_kernel, n_dom, n_rep), out_shape=...  16.9 us
    pallas_call x1, Pallas kernels, on_device(): pl.pallas_call(functools.partial(backward_kernel, n_rep), out_shape=(shap...  13.9 us
    pallas_call x1, Pallas kernels, on_device(): pl.pallas_call(functools.partial(halo_kernel, n_dom), out_shape=(shape((n...  12.1 us
    pallas_call x1, Pallas kernels, on_device(): pl.pallas_call(functools.partial(atom_kernel, n_rep), out_shape=(shape((a...  10.3 us
    unnamed x30, local copies, waits for them, and re-layouts  9.26 us
    pallas_call x1, Pallas kernels, on_device(): pl.pallas_call(forward_kernel, out_shape=shape((n_rep, share, channels),...  3.93 us

profile of v1, /device:TPU:1, one launch (start us, length us, event | category | flops | bytes accessed | tf_op | source)
XLA Modules:
  0.0 67.1 jit_solution(17680146631143430720)
XLA Ops:
  0.6 0.0 copy-start.12
  0.6 0.0 copy-start
  0.7 1.2 %copy-done = bf16[8,256,256]{2,1,0:T(8,128)(2,1)S(1)} copy-done((bf16[8,256,256]{2,1,0:T(8,128)(2,1)S(1)}, bf16[8,256,256]{2,1,0:T(8,128)(2,1)}, u32[]{:S(2)}) %copy-start) | copy-done | bytes 1048600
  1.9 0.0 copy-start.2
  1.9 0.9 %copy-done.2 = bf16[256,256]{1,0:T(8,128)(2,1)S(1)} copy-done((bf16[256,256]{1,0:T(8,128)(2,1)S(1)}, bf16[256,256]{1,0:T(8,128)(2,1)}, u32[]{:S(2)}) %copy-start.2) | copy-done | bytes 131096
  2.8 0.0 copy-start.5
  2.8 0.7 %copy-done.5 = s32[4,128]{1,0:T(4,128)S(1)} copy-done((s32[4,128]{1,0:T(4,128)S(1)}, s32[4,128]{1,0:T(4,128)}, u32[]{:S(2)}) %copy-start.5) | copy-done | bytes 2072
  3.5 0.0 copy-start.7
  3.5 0.7 %copy-done.7 = f32[3,256]{1,0:T(4,128)S(1)} copy-done((f32[3,256]{1,0:T(4,128)S(1)}, f32[3,256]{1,0:T(4,128)}, u32[]{:S(2)}) %copy-start.7) | copy-done | bytes 3096
  4.1 0.0 copy-start.3
  4.2 0.0 copy-start.1
  4.2 12.1 %halo.1 = (bf16[6,8,128,256]{3,2,1,0:T(8,128)(2,1)S(1)}, f32[6,3,128]{2,1,0:T(4,128)S(1)}) custom-call(bf16[256,256]{1,0:T(8,128)(2,1)S(1)} %copy-done.2, f32[3,256]{1,0:T(4,128)S(1)} %copy-done.7, s32[4,128]{1,0:T(4,128)S(1)} %copy-done.5, bf16[8,256,256]{2,1,0:T(8,128)(2,1)S(1)} %copy-done), custom_call_target="tpu_custom_call" | custom-call | tf_op jit(solution)/shard_map/halo/pallas_call | solution.py:417
  16.2 0.0 copy-start.4
  16.3 0.7 %copy-done.4 = s32[3,48]{1,0:T(4,128)S(1)} copy-done((s32[3,48]{1,0:T(4,128)S(1)}, s32[3,48]{1,0:T(4,128)}, u32[]{:S(2)}) %copy-start.4) | copy-done | bytes 600
  16.9 0.0 copy-start.8
  16.9 0.7 copy-done.8
  17.6 0.0 copy-start.9
  17.6 0.7 copy-done.9
  18.2 0.0 copy-start.10
  18.2 0.7 copy-done.10
  18.9 0.0 copy-start.11
  18.9 0.7 copy-done.11
  19.6 3.9 %forward_pairs.1.msg = bf16[4,64,256]{2,1,0:T(8,128)(2,1)S(1)} custom-call(f32[8]{0:T(128)S(1)} %copy-done.8, s32[48]{0:T(128)S(1)} %copy-done.9, s32[48]{0:T(128)S(1)} %copy-done.10, s32[48]{0:T(128)S(1)} %copy-done.11, s32[3,48]{1,0:T(4,128)S(1)} %copy-done.4, f32[6,3,128]{2,1,0:T(4,128)S(1)} %get-tuple-element.12.tiles, ...), custom_call_target="tpu_custom_call" | custom-call | tf_op jit(solution)/shard_map/forward_pairs/pallas_call | solution.py:431
  23.5 0.0 copy-done.12
  23.5 0.0 copy-done.3
  23.5 0.0 copy-start.6
  23.5 10.3 %atoms.1 = (bf16[256,256]{1,0:T(8,128)(2,1)S(1)}, bf16[256,256]{1,0:T(8,128)(2,1)S(1)}, bf16[2,128,256]{2,1,0:T(8,128)(2,1)S(1)}) custom-call(bf16[4,64,256]{2,1,0:T(8,128)(2,1)S(1)} %forward_pairs.1.msg, bf16[256,256]{1,0:T(8,128)(2,1)S(1)} %copy-done.3, f32[1,256]{1,0:T(1,128)S(1)} %bitcast.1), custom_call_target="tpu_custom_call" | custom-call | tf_op jit(solution)/shard_map/atoms/pallas_call | solution.py:441
  33.8 0.0 copy-done.1
  33.8 13.9 %backward_pairs.1 = (bf16[6,2,128,128]{3,2,1,0:T(8,128)(2,1)S(1)}, f32[6,16,128]{2,1,0:T(8,128)S(1)}, f32[8,32,64]{2,1,0:T(8,128)S(1)}) custom-call(f32[8]{0:T(128)S(1)} %copy-done.8, s32[48]{0:T(128)S(1)} %copy-done.9, s32[48]{0:T(128)S(1)} %copy-done.10, s32[48]{0:T(128)S(1)} %copy-done.11, s32[3,48]{1,0:T(4,128)S(1)} %copy-done.4, ...), custom_call_target="tpu_custom_call" | custom-call | tf_op jit(solution)/shard_map/backward_pairs/pallas_call | solution.py:453
  47.7 0.0 copy-done.6
  47.7 16.9 %return_gradients.1 = (bf16[256,256]{1,0:T(8,128)(2,1)S(1)}, f32[3,256]{1,0:T(4,128)S(1)}, f32[6,256]{1,0:T(8,128)S(1)}, f32[32,64]{1,0:T(8,128)S(1)}) custom-call(bf16[6,2,128,128]{3,2,1,0:T(8,128)(2,1)S(1)} %get-tuple-element.17.gfeat, f32[6,16,128]{2,1,0:T(8,128)S(1)} %get-tuple-element.18.side, f32[8,32,64]{2,1,0:T(8,128)S(1)} %get-tuple-element.19.mix, ...), custom_call_target="tpu_custom_call" | custom-call | tf_op jit(solution)/shard_map/return_gradients/pallas_call | solution.py:469
  64.6 0.7 copy.19
  65.3 0.6 copy.20
  65.9 0.6 copy.21
  66.5 0.6 copy.22
Async XLA Ops:
  0.6 22.9 %copy-start.12 = (f32[256]{0:T(256)S(1)}, f32[256]{0:T(256)}, u32[]{:S(2)}) copy-start(f32[256]{0:T(256)} %param.15) | copy-start | bytes 3076
  0.6 1.2 %copy-start = (bf16[8,256,256]{2,1,0:T(8,128)(2,1)S(1)}, bf16[8,256,256]{2,1,0:T(8,128)(2,1)}, u32[]{:S(2)}) copy-start(bf16[8,256,256]{2,1,0:T(8,128)(2,1)} %radial.3) | copy-start | bytes 3145732
  1.9 0.9 %copy-start.2 = (bf16[256,256]{1,0:T(8,128)(2,1)S(1)}, bf16[256,256]{1,0:T(8,128)(2,1)}, u32[]{:S(2)}) copy-start(bf16[256,256]{1,0:T(8,128)(2,1)} %feat.1) | copy-start | bytes 393220
  2.8 0.7 %copy-start.5 = (s32[4,128]{1,0:T(4,128)S(1)}, s32[4,128]{1,0:T(4,128)}, u32[]{:S(2)}) copy-start(s32[4,128]{1,0:T(4,128)} %rows.3) | copy-start | bytes 6148
  3.5 0.7 %copy-start.7 = (f32[3,256]{1,0:T(4,128)S(1)}, f32[3,256]{1,0:T(4,128)}, u32[]{:S(2)}) copy-start(f32[3,256]{1,0:T(4,128)} %pos.1) | copy-start | bytes 9220
  4.1 19.4 %copy-start.3 = (bf16[256,256]{1,0:T(8,128)(2,1)S(1)}, bf16[256,256]{1,0:T(8,128)(2,1)}, u32[]{:S(2)}) copy-start(bf16[256,256]{1,0:T(8,128)(2,1)} %mixing.1) | copy-start | bytes 393220
  4.2 29.7 %copy-start.1 = (bf16[8,256,256]{2,1,0:T(8,128)(2,1)S(1)}, bf16[8,256,256]{2,1,0:T(8,128)(2,1)}, u32[]{:S(2)}) copy-start(bf16[8,256,256]{2,1,0:T(8,128)(2,1)} %radial.3) | copy-start | bytes 3145732
  16.2 0.7 %copy-start.4 = (s32[3,48]{1,0:T(4,128)S(1)}, s32[3,48]{1,0:T(4,128)}, u32[]{:S(2)}) copy-start(s32[3,48]{1,0:T(4,128)} %image.3) | copy-start | bytes 1732
  16.9 0.7 copy-start.8
  17.6 0.7 copy-start.9
  18.2 0.7 copy-start.10
  18.9 0.7 copy-start.11
  23.5 24.2 %copy-start.6 = (s32[4,128]{1,0:T(4,128)S(1)}, s32[4,128]{1,0:T(4,128)}, u32[]{:S(2)}) copy-start(s32[4,128]{1,0:T(4,128)} %rows.3) | copy-start | bytes 6148

commit v2 on v1

--- a/solution.py
+++ b/solution.py
@@ -15,7 +15,7 @@
 BF16 = jnp.bfloat16
 MESH = pl.DeviceIdType.MESH
 VMEM = pl.BlockSpec(memory_space=pltpu.VMEM)
-SMEM = pl.BlockSpec(memory_space=pltpu.SMEM)
+HBM = pl.BlockSpec(memory_space=pltpu.HBM)
 
 
 def nt(a, b):
@@ -38,23 +38,37 @@
     return hi, mid, low
 
 
-def halo_kernel(n_dom, feat, pos, rows, radial, mapped, tiles, sendf, sendp, recvf, recvp,
-                sf, sp, rf, rp):
+def front_kernel(n_dom, n_rep, feat_h, pos_h, rows_h, radial_h, mixing_h, readout_h, decay_h, home_h, other_h,
+                 kind_h, image_h, mapped, tiles, kern_t, packed, slope, adjoint, radial,
+                 feat, pos, rows, mixing, readout, decay, home, other, kind, image,
+                 sendf, sendp, recvf, recvp, col, acc, msg, recv, pk, sl,
+                 load, sf, sp, rf, rp, s1, r1, s2, r2, s3, r3):
     d = lax.axis_index("dom")
     r = lax.axis_index("rep")
+    loads = [pltpu.make_async_copy(src, dst, load.at[i]) for i, (src, dst) in enumerate((
+        (rows_h, rows), (feat_h, feat), (pos_h, pos), (radial_h, radial), (decay_h, decay), (home_h, home),
+        (other_h, other), (kind_h, kind), (image_h, image), (mixing_h, mixing), (readout_h, readout)))]
+    for copy in loads:
+        copy.start()
     barrier = pltpu.get_barrier_semaphore()
     for o in OFFSETS:
         pl.semaphore_signal(barrier, inc=1, device_id={"dom": lax.rem(d + o + n_dom, n_dom), "rep": r},
                             device_id_type=MESH)
+    peers = [lax.rem(r + i, n_rep) for i in range(1, n_rep)]
+    for q in peers:
+        pl.semaphore_signal(barrier, inc=1, device_id={"dom": d, "rep": q}, device_id_type=MESH)
     atoms = feat.shape[0]
+    own = atoms // TILE
     iota = lax.broadcasted_iota(jnp.int32, (atoms, TILE), 0)
-    for t in range(4):
+    for copy in loads[:3]:
+        copy.wait()
+    copies = []
+    for t, o in enumerate(OFFSETS):
         hot = (iota == rows[t:t + 1, :]).astype(F32)
         sendf[t] = tn(hot.astype(BF16), feat[...]).astype(BF16)
         sendp[t] = jnp.dot(pos[...], hot, precision=lax.Precision.HIGHEST, preferred_element_type=F32)
-    pl.semaphore_wait(barrier, 4)
-    copies = []
-    for t, o in enumerate(OFFSETS):
+        if t == 0:
+            pl.semaphore_wait(barrier, 4 + n_rep - 1)
         to = {"dom": lax.rem(d + o + n_dom, n_dom), "rep": r}
         cf = pltpu.make_async_remote_copy(sendf.at[t], recvf.at[t], sf.at[t], rf.at[t],
                                           device_id=to, device_id_type=MESH)
@@ -63,9 +77,16 @@
         cf.start()
         cp.start()
         copies.append((cf, cp))
-    own = atoms // TILE
+
+    def columns(j):
+        for c in range(3):
+            col[j, c] = jnp.transpose(jnp.broadcast_to(tiles[j][c:c + 1, :], (TILE, TILE)))
+
+    for copy in loads[3:]:
+        copy.wait()
     for j in range(own):
         tiles[j] = pos[:, j * TILE:(j + 1) * TILE]
+        columns(j)
 
     def local(k, _):
         res = mm(feat[...], radial[k]).astype(BF16)
@@ -79,59 +100,41 @@
             copies[t][0].wait_recv()
             copies[t][1].wait_recv()
             tiles[own + t] = recvp[t]
-
-        def far(k, _):
+            columns(own + t)
+
+        def distant(k, _):
             both = jnp.concatenate([recvf[2 * h], recvf[2 * h + 1]], axis=0)
             res = mm(both, radial[k]).astype(BF16)
             mapped[own + 2 * h, k] = res[:TILE]
             mapped[own + 2 * h + 1, k] = res[TILE:]
             return 0
 
-        lax.fori_loop(0, radial.shape[0], far, 0)
-    for cf, cp in copies:
-        cf.wait_send()
-        cp.wait_send()
-
-
-def forward_kernel(decay, home, other, kind, image, tiles, mapped, out, near, acc):
-    for i in range(2):
-        for c in range(3):
-            near[i, c] = jnp.transpose(jnp.broadcast_to(tiles[i][c:c + 1, :], (TILE, TILE)))
+        lax.fori_loop(0, radial.shape[0], distant, 0)
+
     acc[...] = jnp.zeros_like(acc)
-
-    def body(g, _):
-        found = []
+    pairs = home.shape[0]
+
+    def forward(g, _):
+        left, right = [], []
         for u in range(GROUP):
             p = g * GROUP + u
             h, o, k = home[p], other[p], kind[p]
-            rate = decay[k]
             row = tiles[o]
             d2 = None
             for c in range(3):
-                sep = (row[c:c + 1, :] + image[c, p].astype(F32) * CELL) - near[h, c]
+                sep = (row[c:c + 1, :] + image[c, p].astype(F32) * CELL) - col[h, c]
                 d2 = sep * sep if d2 is None else d2 + sep * sep
-            kern = jnp.exp(d2 * (-rate)).astype(BF16)
-            found.append((h, mm(kern, mapped[o, k])))
-        for h, m in found:
-            acc[h] += m
-        return 0
-
-    lax.fori_loop(0, home.shape[0] // GROUP, body, 0)
-    share = out.shape[1]
-    per = TILE // share
-    for i in range(2):
-        for q in range(per):
-            out[i * per + q] = acc[i, q * share:(q + 1) * share, :].astype(BF16)
-
-
-def atom_kernel(n_rep, msg, mixing, readout, packed, slope, adjoint, recv, pk, sl, s1, r1, s2, r2, s3, r3):
-    d = lax.axis_index("dom")
-    r = lax.axis_index("rep")
-    barrier = pltpu.get_barrier_semaphore()
-    peers = [lax.rem(r + i, n_rep) for i in range(1, n_rep)]
-    for q in peers:
-        pl.semaphore_signal(barrier, inc=1, device_id={"dom": d, "rep": q}, device_id_type=MESH)
-    pl.semaphore_wait(barrier, n_rep - 1)
+            kern = jnp.exp(d2 * (-decay[k]))
+            left.append(jnp.concatenate(
+                [(kern * (h == i).astype(F32)).astype(BF16) for i in range(own)], axis=0))
+            right.append(mapped[o, k])
+        acc[...] += mm(jnp.concatenate(left, axis=1), jnp.concatenate(right, axis=0))
+        return 0
+
+    lax.fori_loop(0, pairs // GROUP, forward, 0)
+    share = atoms // n_rep
+    for q in range(n_rep):
+        msg[q] = acc[q * share:(q + 1) * share, :].astype(BF16)
 
     def push(src, dst, ss, rs, q):
         copy = pltpu.make_async_remote_copy(src, dst, ss, rs, device_id={"dom": d, "rep": q},
@@ -143,40 +146,61 @@
         pltpu.make_async_remote_copy(dst, dst, ss, rs, device_id={"dom": d, "rep": q},
                                      device_id_type=MESH).wait_recv()
 
+    def transposed(g, _):
+        for u in range(GROUP):
+            p = g * GROUP + u
+            h, o, k = home[p], other[p], kind[p]
+            row = tiles[h]
+            d2 = None
+            for c in range(3):
+                sep = col[o, c] - (row[c:c + 1, :] - image[c, p].astype(F32) * CELL)
+                d2 = sep * sep if d2 is None else d2 + sep * sep
+            kern_t[p] = jnp.exp(d2 * (-decay[k]))
+        return 0
+
     sent = [push(msg.at[q], recv.at[r], s1.at[i], r1.at[r], q) for i, q in enumerate(peers)]
+    half = pairs // GROUP // 2
+    lax.fori_loop(0, half, transposed, 0)
     total = msg[r].astype(F32)
     for i, q in enumerate(peers):
         take(recv.at[q], s1.at[i], r1.at[q], q)
         total = total + recv[q].astype(F32)
     low = total.astype(BF16)
     pk[r] = low
-    sent += [push(pk.at[r], pk.at[r], s2.at[i], r2.at[r], q) for i, q in enumerate(peers)]
     mixed = mm(low, mixing[...])
     sig = jax.nn.sigmoid(mixed)
     sl[r] = (readout[...] * sig * (1.0 + mixed * (1.0 - sig))).astype(BF16)
     sent += [push(sl.at[r], sl.at[r], s3.at[i], r3.at[r], q) for i, q in enumerate(peers)]
+    sent += [push(pk.at[r], pk.at[r], s2.at[i], r2.at[r], q) for i, q in enumerate(peers)]
+    lax.fori_loop(half, pairs // GROUP, transposed, 0)
     for i, q in enumerate(peers):
         take(sl.at[q], s3.at[i], r3.at[q], q)
     full = sl[...].reshape(-1, mixing.shape[0])
     slope[...] = full
     adj = nt(full, mixing[...]).astype(BF16)
-    for j in range(adjoint.shape[0]):
+    for j in range(own):
         adjoint[j] = adj[j * TILE:(j + 1) * TILE]
     for i, q in enumerate(peers):
         take(pk.at[q], s2.at[i], r2.at[q], q)
     packed[...] = pk[...].reshape(-1, mixing.shape[0])
+    for cf, cp in copies:
+        cf.wait_send()
+        cp.wait_send()
     for copy in sent:
         copy.wait_send()
 
 
-def backward_kernel(n_rep, decay, home, other, kind, image, tiles, mapped, adjoint, radial, packed, slope,
-                    gfeat, side, mix, far, moments, first, second, acc):
+def backward_kernel(n_rep, decay_h, home_h, other_h, kind_h, image_h, tiles, mapped, kern_t, adjoint, radial,
+                    packed, slope, gfeat, side, mix, decay, home, other, kind, image, moments, first, second,
+                    acc, load):
+    loads = [pltpu.make_async_copy(src, dst, load.at[i]) for i, (src, dst) in enumerate((
+        (decay_h, decay), (home_h, home), (other_h, other), (kind_h, kind), (image_h, image)))]
+    for copy in loads:
+        copy.start()
     n_ext = tiles.shape[0]
     for j in range(n_ext):
         pos = tiles[j]
         x, y, z = pos[0:1, :], pos[1:2, :], pos[2:3, :]
-        for c in range(3):
-            far[j, c] = jnp.transpose(jnp.broadcast_to(pos[c:c + 1, :], (TILE, TILE)))
         zero = jnp.zeros((2, TILE), F32)
         one_rows = jnp.concatenate([x, y, z, x, x, y, zero], axis=0)
         two_rows = jnp.concatenate([x, y, z, y, z, z, zero], axis=0)
@@ -208,6 +232,9 @@
         virial = -0.5 * (quad - a * lin2 - b * lin1 + a * b * one)
         return jnp.concatenate([force, virial], axis=0)
 
+    for copy in loads:
+        copy.wait()
+
     def body(g, _):
         found = []
         for u in range(GROUP):
@@ -215,12 +242,7 @@
             h, o, k = home[p], other[p], kind[p]
             rate = decay[k]
             shift = [image[c, p].astype(F32) * CELL for c in range(3)]
-            row = tiles[h]
-            d2 = None
-            for c in range(3):
-                sep = far[o, c] - (row[c:c + 1, :] - shift[c])
-                d2 = sep * sep if d2 is None else d2 + sep * sep
-            kern = jnp.exp(d2 * (-rate))
+            kern = kern_t[p]
             adj = adjoint[h]
             weight = (-2.0 * rate) * kern * nt(mapped[o, k], adj)
             back = mm(kern.astype(BF16), adj).astype(BF16)
@@ -397,6 +419,15 @@
     cq.wait_send()
 
 
+def copy_out(a, b, c, d, a_h, b_h, c_h, d_h, sem):
+    copies = [pltpu.make_async_copy(src, dst, sem.at[i])
+              for i, (src, dst) in enumerate(((a, a_h), (b, b_h), (c, c_h), (d, d_h)))]
+    for copy in copies:
+        copy.start()
+    for copy in copies:
+        copy.wait()
+
+
 def on_device(n_dom, n_rep, features, positions, radial, mixing, readout, decay, send_rows, pair_home,
               pair_other, pair_kind, pair_image):
     atoms, channels = features.shape
@@ -414,59 +445,54 @@
     def shape(dims, dtype):
         return jax.ShapeDtypeStruct(dims, dtype)
 
-    mapped, tiles = pl.pallas_call(
-        functools.partial(halo_kernel, n_dom),
-        out_shape=(shape((n_ext, kinds, TILE, channels), BF16), shape((n_ext, 3, TILE), F32)),
-        in_specs=[VMEM] * 4,
-        out_specs=(VMEM, VMEM),
+    def pair_tables():
+        return [pltpu.SMEM(decay.shape, F32)] + [
+            pltpu.SMEM(a.shape, jnp.int32) for a in (pair_home, pair_other, pair_kind, pair_image)]
+
+    readout_row = readout.reshape(1, channels)
+    mapped, tiles, kern_t, packed, slope, adjoint, radial_near = pl.pallas_call(
+        functools.partial(front_kernel, n_dom, n_rep),
+        out_shape=(shape((n_ext, kinds, TILE, channels), BF16), shape((n_ext, 3, TILE), F32),
+                   shape((pair_home.shape[0], TILE, TILE), F32), shape((atoms, channels), BF16),
+                   shape((atoms, channels), BF16), shape((own, TILE, channels), BF16),
+                   shape(radial.shape, BF16)),
+        in_specs=[HBM] * 11,
+        out_specs=(VMEM,) * 7,
         scratch_shapes=[
+            pltpu.VMEM(features.shape, BF16), pltpu.VMEM(positions.shape, F32),
+            pltpu.VMEM(send_rows.shape, jnp.int32),
+            pltpu.VMEM(mixing.shape, BF16), pltpu.VMEM(readout_row.shape, F32), *pair_tables(),
             pltpu.VMEM((4, TILE, channels), BF16), pltpu.VMEM((4, 3, TILE), F32),
             pltpu.VMEM((4, TILE, channels), BF16), pltpu.VMEM((4, 3, TILE), F32),
-            dma((4,)), dma((4,)), dma((4,)), dma((4,)),
+            pltpu.VMEM((n_ext, 3, TILE, TILE), F32), pltpu.VMEM((atoms, channels), F32),
+            *[pltpu.VMEM((n_rep, share, channels), BF16)] * 4,
+            dma((11,)), dma((4,)), dma((4,)), dma((4,)), dma((4,)), *[dma((n_rep,)) for _ in range(6)],
         ],
         compiler_params=params(0),
-        name="halo",
-    )(features, positions, send_rows, radial)
-
-    message = pl.pallas_call(
-        forward_kernel,
-        out_shape=shape((n_rep, share, channels), BF16),
-        in_specs=[SMEM] * 5 + [VMEM] * 2,
-        out_specs=VMEM,
-        scratch_shapes=[pltpu.VMEM((2, 3, TILE, TILE), F32), pltpu.VMEM((own, TILE, channels), F32)],
-        compiler_params=params(),
-        name="forward_pairs",
-    )(decay, pair_home, pair_other, pair_kind, pair_image, tiles, mapped)
-
-    packed, slope, adjoint = pl.pallas_call(
-        functools.partial(atom_kernel, n_rep),
-        out_shape=(shape((atoms, channels), BF16), shape((atoms, channels), BF16),
-                   shape((own, TILE, channels), BF16)),
-        in_specs=[VMEM] * 3,
-        out_specs=(VMEM,) * 3,
-        scratch_shapes=[pltpu.VMEM((n_rep, share, channels), BF16)] * 3
-        + [dma((n_rep,)) for _ in range(6)],
-        compiler_params=params(1),
-        name="atoms",
-    )(message, mixing, readout.reshape(1, channels))
+        name="front",
+    )(*[pltpu.with_memory_space_constraint(a, pltpu.HBM) for a in (
+        features, positions, send_rows, radial, mixing, readout_row, decay, pair_home, pair_other, pair_kind,
+        pair_image)])
 
     gfeat, side, mix = pl.pallas_call(
         functools.partial(backward_kernel, n_rep),
         out_shape=(shape((n_ext, 2, TILE, channels // 2), BF16), shape((n_ext, 16, TILE), F32),
                    shape((n_dom, channels // n_dom, channels // n_rep), F32)),
-        in_specs=[SMEM] * 5 + [VMEM] * 6,
+        in_specs=[HBM] * 5 + [VMEM] * 7,
         out_specs=(VMEM,) * 3,
         scratch_shapes=[
-            pltpu.VMEM((n_ext, 3, TILE, TILE), F32), pltpu.VMEM((n_ext, 80, TILE), BF16),
+            *pair_tables(), pltpu.VMEM((n_ext, 80, TILE), BF16),
             pltpu.VMEM((n_ext, 8, TILE), F32), pltpu.VMEM((n_ext, 8, TILE), F32),
-            pltpu.VMEM((n_ext, TILE, channels), F32),
+            pltpu.VMEM((n_ext, TILE, channels), F32), dma((5,)),
         ],
         compiler_params=params(),
         name="backward_pairs",
-    )(decay, pair_home, pair_other, pair_kind, pair_image, tiles, mapped, adjoint, radial, packed, slope)
+    )(*[pltpu.with_memory_space_constraint(a, pltpu.HBM) for a in (
+        decay, pair_home, pair_other, pair_kind, pair_image)],
+      tiles, mapped, kern_t, adjoint, radial_near, packed, slope)
 
     mix_rows, mix_cols = channels // n_dom, channels // n_rep
-    return pl.pallas_call(
+    results = pl.pallas_call(
         functools.partial(return_kernel, n_dom, n_rep),
         out_shape=(shape((atoms, channels), BF16), shape((3, atoms), F32), shape((6, atoms), F32),
                    shape((mix_rows, mix_cols), F32)),
@@ -482,6 +508,15 @@
         compiler_params=params(2),
         name="return_gradients",
     )(gfeat, side, mix, send_rows)
+    return pl.pallas_call(
+        copy_out,
+        out_shape=tuple(shape(a.shape, a.dtype) for a in results),
+        in_specs=[VMEM] * 4,
+        out_specs=(HBM,) * 4,
+        scratch_shapes=[dma((4,))],
+        compiler_params=pltpu.CompilerParams(vmem_limit_bytes=4 << 20),
+        name="copy_out",
+    )(*results)
 
 
 def solution(mesh):

time: 67.4 us -> 58 us (0.86)
  local copies, waits for them, and re-layouts: 9.26 us -> 0.01 us
    unnamed x30 -> x2, local copies, waits for them, and re-layouts: 9.26 us -> 0.01 us
    pallas_call x3 -> x2, Pallas kernels: 26.3 us -> 26.5 us  [the longest x1 25.8 us: on_device(): pl.pallas_call(functools.partial(front_kernel, n_dom, n_rep), out_shape=(...]
where the time goes in v2:
time: 58 us; the launch traced here: 57.8 us
  Pallas kernels  57.1 us (98%)
  between operations  0.67 us (1%)
    pallas_call x1, Pallas kernels, on_device(): pl.pallas_call(functools.partial(front_kernel, n_dom, n_rep), out_shape=(...  25.8 us
    pallas_call x1, Pallas kernels, on_device(): pl.pallas_call(functools.partial(return_kernel, n_dom, n_rep), out_shape=...  16.9 us
    pallas_call x1, Pallas kernels, on_device(): pl.pallas_call(functools.partial(backward_kernel, n_rep), out_shape=(shap...  13.7 us

profile of v2, /device:TPU:1, one launch (start us, length us, event | category | flops | bytes accessed | tf_op | source)
XLA Modules:
  0.0 57.8 jit_solution(368418123493625398)
XLA Ops:
  0.6 25.8 %front.1 = (bf16[6,8,128,256]{3,2,1,0:T(8,128)(2,1)S(1)}, f32[6,3,128]{2,1,0:T(4,128)S(1)}, f32[48,128,128]{2,1,0:T(8,128)S(1)}, bf16[256,256]{1,0:T(8,128)(2,1)...) custom-call(bf16[256,256]{1,0:T(8,128)(2,1)} %feat_h.1, ...), custom_call_target="tpu_custom_call" | custom-call | tf_op jit(solution)/shard_map/front/pallas_call | solution.py:453
  26.4 0.0 copy-start
  26.5 13.7 %backward_pairs.1 = (bf16[6,2,128,128]{3,2,1,0:T(8,128)(2,1)S(1)}, f32[6,16,128]{2,1,0:T(8,128)S(1)}, f32[8,32,64]{2,1,0:T(8,128)S(1)}) custom-call(f32[8]{0:T(128)} %decay_h.3, s32[48]{0:T(128)} %home_h.3, s32[48]{0:T(128)} %other_h.3, s32[48]{0:T(128)} %kind_h.3, s32[3,48]{1,0:T(4,128)} %image_h.3, f32[6,3,128]{2,1,0:T(4,128)S(1)} %get-tuple-element.18.tiles, ...), custom_call_target="tpu_custom_call" | custom-call | tf_op jit(solution)/shard_map/backward_pairs/pallas_call | solution.py:477
  40.2 0.0 copy-done
  40.2 16.9 %return_gradients.1 = (bf16[256,256]{1,0:T(8,128)(2,1)S(1)}, f32[3,256]{1,0:T(4,128)S(1)}, f32[6,256]{1,0:T(8,128)S(1)}, f32[32,64]{1,0:T(8,128)S(1)}) custom-call(bf16[6,2,128,128]{3,2,1,0:T(8,128)(2,1)S(1)} %get-tuple-element.25.gfeat, f32[6,16,128]{2,1,0:T(8,128)S(1)} %get-tuple-element.26.side, f32[8,32,64]{2,1,0:T(8,128)S(1)} %get-tuple-element.27.mix, ...), custom_call_target="tpu_custom_call" | custom-call | tf_op jit(solution)/shard_map/return_gradients/pallas_call | solution.py:495
  57.1 0.7 %copy_out.1 = (bf16[256,256]{1,0:T(8,128)(2,1)}, f32[3,256]{1,0:T(4,128)}, f32[6,256]{1,0:T(8,128)}, f32[32,64]{1,0:T(8,128)}) custom-call(bf16[256,256]{1,0:T(8,128)(2,1)S(1)} %get-tuple-element.28.a, f32[3,256]{1,0:T(4,128)S(1)} %get-tuple-element.29.b, f32[6,256]{1,0:T(8,128)S(1)} %get-tuple-element.30.c, f32[32,64]{1,0:T(8,128)S(1)} %get-tuple-element.31.d), custom_call_target="tpu_custom_call" | custom-call | tf_op jit(solution)/shard_map/copy_out/pallas_call | solution.py:511
Async XLA Ops:
  26.4 13.8 %copy-start = (s32[4,128]{1,0:T(4,128)S(1)}, s32[4,128]{1,0:T(4,128)}, u32[]{:S(2)}) copy-start(s32[4,128]{1,0:T(4,128)} %rows.1) | copy-start | bytes 6148

commit v3 on v2

--- a/solution.py
+++ b/solution.py
@@ -11,6 +11,7 @@
 OFFSETS = (1, -1, 2, -2)
 CELL = 2.0
 GROUP = 4
+BACK_GROUP = 8
 F32 = jnp.float32
 BF16 = jnp.bfloat16
 MESH = pl.DeviceIdType.MESH
@@ -42,7 +43,7 @@
                  kind_h, image_h, mapped, tiles, kern_t, packed, slope, adjoint, radial,
                  feat, pos, rows, mixing, readout, decay, home, other, kind, image,
                  sendf, sendp, recvf, recvp, col, acc, msg, recv, pk, sl,
-                 load, sf, sp, rf, rp, s1, r1, s2, r2, s3, r3):
+                 load, sf, sp, rf, rp, s4, r4, s5, r5, s1, r1, s2, r2, s3, r3):
     d = lax.axis_index("dom")
     r = lax.axis_index("rep")
     loads = [pltpu.make_async_copy(src, dst, load.at[i]) for i, (src, dst) in enumerate((
@@ -51,7 +52,10 @@
     for copy in loads:
         copy.start()
     barrier = pltpu.get_barrier_semaphore()
-    for o in OFFSETS:
+    c = lax.rem(r, 2)
+    partner = {"dom": d, "rep": r + 1 - 2 * c}
+    steps = (c + 1, -(c + 1))
+    for o in steps:
         pl.semaphore_signal(barrier, inc=1, device_id={"dom": lax.rem(d + o + n_dom, n_dom), "rep": r},
                             device_id_type=MESH)
     peers = [lax.rem(r + i, n_rep) for i in range(1, n_rep)]
@@ -63,20 +67,21 @@
     for copy in loads[:3]:
         copy.wait()
     copies = []
-    for t, o in enumerate(OFFSETS):
-        hot = (iota == rows[t:t + 1, :]).astype(F32)
-        sendf[t] = tn(hot.astype(BF16), feat[...]).astype(BF16)
-        sendp[t] = jnp.dot(pos[...], hot, precision=lax.Precision.HIGHEST, preferred_element_type=F32)
-        if t == 0:
-            pl.semaphore_wait(barrier, 4 + n_rep - 1)
+    for q, o in enumerate(steps):
+        t = 2 * c + q
+        hot = (iota == rows[pl.ds(t, 1), :]).astype(F32)
+        sendf[q] = tn(hot.astype(BF16), feat[...]).astype(BF16)
+        sendp[q] = jnp.dot(pos[...], hot, precision=lax.Precision.HIGHEST, preferred_element_type=F32)
+        if q == 0:
+            pl.semaphore_wait(barrier, 2 + n_rep - 1)
         to = {"dom": lax.rem(d + o + n_dom, n_dom), "rep": r}
-        cf = pltpu.make_async_remote_copy(sendf.at[t], recvf.at[t], sf.at[t], rf.at[t],
+        cf = pltpu.make_async_remote_copy(sendf.at[q], recvf.at[t], sf.at[q], rf.at[t],
                                           device_id=to, device_id_type=MESH)
-        cp = pltpu.make_async_remote_copy(sendp.at[t], recvp.at[t], sp.at[t], rp.at[t],
+        cp = pltpu.make_async_remote_copy(sendp.at[q], recvp.at[t], sp.at[q], rp.at[t],
                                           device_id=to, device_id_type=MESH)
         cf.start()
         cp.start()
-        copies.append((cf, cp))
+        copies += [cf, cp]
 
     def columns(j):
         for c in range(3):
@@ -95,21 +100,35 @@
         return 0
 
     lax.fori_loop(0, radial.shape[0], local, 0)
-    for h in range(2):
-        for t in (2 * h, 2 * h + 1):
-            copies[t][0].wait_recv()
-            copies[t][1].wait_recv()
-            tiles[own + t] = recvp[t]
-            columns(own + t)
-
-        def distant(k, _):
-            both = jnp.concatenate([recvf[2 * h], recvf[2 * h + 1]], axis=0)
-            res = mm(both, radial[k]).astype(BF16)
-            mapped[own + 2 * h, k] = res[:TILE]
-            mapped[own + 2 * h + 1, k] = res[TILE:]
-            return 0
-
-        lax.fori_loop(0, radial.shape[0], distant, 0)
+    def distant(base, k):
+        both = recvf[pl.ds(base, 2)].reshape(2 * TILE, -1)
+        res = mm(both, radial[k]).astype(BF16)
+        mapped[own + base, k] = res[:TILE]
+        mapped[own + base + 1, k] = res[TILE:]
+
+    def unpack(base):
+        for q in range(2):
+            tiles[own + base + q] = recvp[base + q]
+            columns(own + base + q)
+        lax.fori_loop(0, radial.shape[0], lambda k, _: (distant(base, k), 0)[1], 0)
+
+    relays = []
+    for q in range(2):
+        t = 2 * c + q
+        copies[2 * q].wait_recv()
+        copies[2 * q + 1].wait_recv()
+        relays.append(pltpu.make_async_remote_copy(recvf.at[t], recvf.at[t], s4.at[q], r4.at[t],
+                                                   device_id=partner, device_id_type=MESH))
+        relays.append(pltpu.make_async_remote_copy(recvp.at[t], recvp.at[t], s5.at[q], r5.at[t],
+                                                   device_id=partner, device_id_type=MESH))
+        relays[-2].start()
+        relays[-1].start()
+    unpack(2 * c)
+    for q in range(2):
+        t = 2 * (1 - c) + q
+        for dst, ss, rs in ((recvf.at[t], s4.at[q], r4.at[t]), (recvp.at[t], s5.at[q], r5.at[t])):
+            pltpu.make_async_remote_copy(dst, dst, ss, rs, device_id=partner, device_id_type=MESH).wait_recv()
+    unpack(2 * (1 - c))
 
     acc[...] = jnp.zeros_like(acc)
     pairs = home.shape[0]
@@ -183,10 +202,7 @@
     for i, q in enumerate(peers):
         take(pk.at[q], s2.at[i], r2.at[q], q)
     packed[...] = pk[...].reshape(-1, mixing.shape[0])
-    for cf, cp in copies:
-        cf.wait_send()
-        cp.wait_send()
-    for copy in sent:
+    for copy in copies + relays + sent:
         copy.wait_send()
 
 
@@ -208,8 +224,9 @@
         second[j] = two_rows
         stack = jnp.concatenate([one_rows * two_rows, one_rows, two_rows], axis=0)
         parts = [v.astype(F32) for v in split3(stack)]
-        moments[j] = jnp.concatenate(
+        table = jnp.concatenate(
             [parts[0], jnp.ones((8, TILE), F32), parts[1], parts[2]], axis=0).astype(BF16)
+        moments[j] = jnp.concatenate([table, table], axis=1)
     acc[...] = jnp.zeros_like(acc)
     side[...] = jnp.zeros_like(side)
     sub = lax.broadcasted_iota(jnp.int32, (8, TILE), 0)
@@ -237,20 +254,23 @@
 
     def body(g, _):
         found = []
-        for u in range(GROUP):
-            p = g * GROUP + u
+        names = []
+        weights = []
+        for u in range(BACK_GROUP):
+            p = g * BACK_GROUP + u
             h, o, k = home[p], other[p], kind[p]
-            rate = decay[k]
-            shift = [image[c, p].astype(F32) * CELL for c in range(3)]
+            names.append((p, h, o, k))
             kern = kern_t[p]
-            adj = adjoint[h]
-            weight = (-2.0 * rate) * kern * nt(mapped[o, k], adj)
-            back = mm(kern.astype(BF16), adj).astype(BF16)
-            part = nt(back, radial[k])
+            weight = (-2.0 * decay[k]) * kern * nt(mapped[o, k], adjoint[h])
             hi = weight.astype(BF16)
             lo = (weight - hi.astype(F32)).astype(BF16)
-            near_res = mm(moments[o], hi) + mm(moments[o], lo)
-            far_res = nt(moments[h], hi) + nt(moments[h], lo)
+            weights.append((hi, lo))
+        for (p, h, o, k), (hi, lo) in zip(names, weights):
+            back = mm(kern_t[p].astype(BF16), adjoint[h]).astype(BF16)
+            part = nt(back, radial[k])
+            shift = [image[c, p].astype(F32) * CELL for c in range(3)]
+            near_res = mm(moments[o], jnp.concatenate([hi, lo], axis=0))
+            far_res = nt(moments[h], jnp.concatenate([hi, lo], axis=1))
             s1 = jnp.where(is_x1, shift[0], jnp.where(is_y1, shift[1], shift[2]))
             s2 = jnp.where(is_x2, shift[0], jnp.where(is_y2, shift[1], shift[2]))
             near_side = combine(near_res, first[h] - s1, second[h] - s2)
@@ -262,7 +282,7 @@
             side[o] += far_side
         return 0
 
-    lax.fori_loop(0, home.shape[0] // GROUP, body, 0)
+    lax.fori_loop(0, home.shape[0] // BACK_GROUP, body, 0)
     for j in range(n_ext):
         for half in range(2):
             gfeat[j, half] = acc[j, :, half * TILE:(half + 1) * TILE].astype(BF16)
@@ -276,13 +296,9 @@
     mix[...] = res.reshape(mix.shape)
 
 
-TILE_CORE = (0, 1, 0, 0, 1, 1)
-TILE_SLOT = (0, 0, 1, 2, 1, 2)
-
-
 def return_kernel(n_dom, n_rep, gfeat, side, mix, rows, out_feat, out_force, out_virial, out_mix,
-                  rf, rs, rm, part, pside, qside,
-                  sem_sf, sem_rf, sem_ss, sem_rs, sem_sm, sem_rm, sem_sp, sem_rp, sem_sq, sem_rq):
+                  gp, gs, sb, ss, rf, rs, rm, part, pside, qside,
+                  sem_gf, sem_hf, sem_gs, sem_hs, sem_sf, sem_rf, sem_ss, sem_rs, sem_sm, sem_rm, sem_sp, sem_rp, sem_sq, sem_rq):
     d = lax.axis_index("dom")
     r = lax.axis_index("rep")
     y = lax.div(r, 2)
@@ -299,8 +315,8 @@
     mine = [(c + 1), -(c + 1)]
     peers = [lax.rem(r + i, n_rep) for i in range(1, n_rep)]
     for o in mine:
-        for q in range(n_rep):
-            hello(dom_at(o), q)
+        for half in range(n_rep // 2):
+            hello(dom_at(o), 2 * half + c)
     for q in peers:
         hello(d, q)
 
@@ -309,27 +325,35 @@
         return 0
 
     lax.fori_loop(1, n_dom, greet, 0)
-    pl.semaphore_wait(barrier, 2 * n_rep + n_rep - 1 + n_dom - 1)
-
+    pl.semaphore_wait(barrier, n_rep + n_rep - 1 + n_dom - 1)
+
+    partner = {"dom": d, "rep": r + 1 - 2 * c}
+    mate = 1 - c
     sends = []
-    for j in (2, 3, 4, 5, 0, 1):
-        for half in range(2):
-            to = half * 2 + TILE_CORE[j]
-            dest = {"dom": d if j < 2 else dom_at(-OFFSETS[j - 2]), "rep": to}
-            slot = TILE_SLOT[j]
-            cf = pltpu.make_async_remote_copy(gfeat.at[j, half], rf.at[slot, r], sem_sf.at[j, half],
-                                              sem_rf.at[slot, r], device_id=dest, device_id_type=MESH)
-            cs = pltpu.make_async_remote_copy(side.at[j], rs.at[slot, r], sem_ss.at[j, half],
-                                              sem_rs.at[slot, r], device_id=dest, device_id_type=MESH)
-            sends.append((j, to, cf, cs))
-            if j < 2:
-                @pl.when(r != to)
-                def _():
-                    cf.start()
-                    cs.start()
-            else:
-                cf.start()
-                cs.start()
+    swaps = []
+    for slot, j in ((1, 2 + 2 * mate), (2, 3 + 2 * mate), (0, mate)):
+        cf = pltpu.make_async_remote_copy(gfeat.at[j], gp.at[slot], sem_gf.at[slot], sem_hf.at[slot],
+                                          device_id=partner, device_id_type=MESH)
+        cs = pltpu.make_async_remote_copy(side.at[j], gs.at[slot], sem_gs.at[slot], sem_hs.at[slot],
+                                          device_id=partner, device_id_type=MESH)
+        cf.start()
+        cs.start()
+        swaps.append((cf, cs))
+        sends += [cf, cs]
+    for (cf, cs), (slot, j) in zip(swaps, ((1, 2 + 2 * c), (2, 3 + 2 * c), (0, c))):
+        cf.wait_recv()
+        cs.wait_recv()
+        sb[slot] = (gfeat[j].astype(F32) + gp[slot].astype(F32)).astype(BF16)
+        ss[slot] = side[j] + gs[slot]
+        for half in ((0, 1) if slot else (1 - y,)):
+            dest = {"dom": dom_at(-mine[slot - 1]) if slot else d, "rep": 2 * half + c}
+            nf = pltpu.make_async_remote_copy(sb.at[slot, half], rf.at[slot, y], sem_sf.at[slot, half],
+                                              sem_rf.at[slot, y], device_id=dest, device_id_type=MESH)
+            ns = pltpu.make_async_remote_copy(ss.at[slot], rs.at[slot, y], sem_ss.at[slot, half],
+                                              sem_rs.at[slot, y], device_id=dest, device_id_type=MESH)
+            nf.start()
+            ns.start()
+            sends += [nf, ns]
 
     def mix_copy(i):
         to = lax.rem(d + i, n_dom)
@@ -346,13 +370,10 @@
         pltpu.make_async_remote_copy(dst, dst, ss, rsem, device_id={"dom": d, "rep": peers[0]},
                                      device_id_type=MESH).wait_recv()
 
-    feat_self = gfeat[c, y].astype(F32)
-    side_self = side[c]
-    for q in peers:
-        take(rf.at[0, q], sem_sf.at[0, 0], sem_rf.at[0, q])
-        take(rs.at[0, q], sem_ss.at[0, 0], sem_rs.at[0, q])
-        feat_self = feat_self + rf[0, q].astype(F32)
-        side_self = side_self + rs[0, q]
+    take(rf.at[0, 1 - y], sem_sf.at[0, 0], sem_rf.at[0, 1 - y])
+    take(rs.at[0, 1 - y], sem_ss.at[0, 0], sem_rs.at[0, 1 - y])
+    feat_self = sb[0, y].astype(F32) + rf[0, 1 - y].astype(F32)
+    side_self = ss[0] + rs[0, 1 - y]
     is_low = c == 0
     zero = jnp.zeros_like(feat_self)
     total = jnp.concatenate([jnp.where(is_low, feat_self, zero), jnp.where(is_low, zero, feat_self)], axis=0)
@@ -365,7 +386,7 @@
         hot = (iota == rows[pl.ds(2 * c + q, 1), :]).astype(F32).astype(BF16)
         slot = 1 + q
         got = None
-        for s in range(n_rep):
+        for s in range(n_rep // 2):
             take(rf.at[slot, s], sem_sf.at[0, 0], sem_rf.at[slot, s])
             take(rs.at[slot, s], sem_ss.at[0, 0], sem_rs.at[slot, s])
             total = total + mm(hot, rf[slot, s])
@@ -399,15 +420,8 @@
     for half in range(2):
         out_feat[:, half * TILE:(half + 1) * TILE] = (
             part[2 * half].astype(F32) + part[2 * half + 1].astype(F32)).astype(BF16)
-    for j, to, cf, cs in sends:
-        if j < 2:
-            @pl.when(r != to)
-            def _():
-                cf.wait_send()
-                cs.wait_send()
-        else:
-            cf.wait_send()
-            cs.wait_send()
+    for copy in sends:
+        copy.wait_send()
 
     def mix_done(i, _):
         mix_copy(i).wait_send()
@@ -462,11 +476,11 @@
             pltpu.VMEM(features.shape, BF16), pltpu.VMEM(positions.shape, F32),
             pltpu.VMEM(send_rows.shape, jnp.int32),
             pltpu.VMEM(mixing.shape, BF16), pltpu.VMEM(readout_row.shape, F32), *pair_tables(),
-            pltpu.VMEM((4, TILE, channels), BF16), pltpu.VMEM((4, 3, TILE), F32),
+            pltpu.VMEM((2, TILE, channels), BF16), pltpu.VMEM((2, 3, TILE), F32),
             pltpu.VMEM((4, TILE, channels), BF16), pltpu.VMEM((4, 3, TILE), F32),
             pltpu.VMEM((n_ext, 3, TILE, TILE), F32), pltpu.VMEM((atoms, channels), F32),
             *[pltpu.VMEM((n_rep, share, channels), BF16)] * 4,
-            dma((11,)), dma((4,)), dma((4,)), dma((4,)), dma((4,)), *[dma((n_rep,)) for _ in range(6)],
+            dma((11,)), *[dma((4,)) for _ in range(8)], *[dma((n_rep,)) for _ in range(6)],
         ],
         compiler_params=params(0),
         name="front",
@@ -481,7 +495,7 @@
         in_specs=[HBM] * 5 + [VMEM] * 7,
         out_specs=(VMEM,) * 3,
         scratch_shapes=[
-            *pair_tables(), pltpu.VMEM((n_ext, 80, TILE), BF16),
+            *pair_tables(), pltpu.VMEM((n_ext, 80, 2 * TILE), BF16),
             pltpu.VMEM((n_ext, 8, TILE), F32), pltpu.VMEM((n_ext, 8, TILE), F32),
             pltpu.VMEM((n_ext, TILE, channels), F32), dma((5,)),
         ],
@@ -499,10 +513,12 @@
         in_specs=[VMEM] * 4,
         out_specs=(VMEM,) * 4,
         scratch_shapes=[
-            pltpu.VMEM((3, n_rep, TILE, channels // 2), BF16), pltpu.VMEM((3, n_rep, 16, TILE), F32),
+            pltpu.VMEM((3, 2, TILE, channels // 2), BF16), pltpu.VMEM((3, 16, TILE), F32),
+            pltpu.VMEM((3, 2, TILE, channels // 2), BF16), pltpu.VMEM((3, 16, TILE), F32),
+            pltpu.VMEM((3, 2, TILE, channels // 2), BF16), pltpu.VMEM((3, 2, 16, TILE), F32),
             pltpu.VMEM((n_dom, mix_rows, mix_cols), F32), pltpu.VMEM((n_rep, atoms, channels // 2), BF16),
             pltpu.VMEM((16, atoms), F32), pltpu.VMEM((16, atoms), F32),
-            dma((n_ext, 2)), dma((3, n_rep)), dma((n_ext, 2)), dma((3, n_rep)),
+            *[dma((3,)) for _ in range(4)], *[dma((3, 2)) for _ in range(4)],
             dma((n_dom,)), dma((n_dom,)), dma((n_rep,)), dma((n_rep,)), dma, dma,
         ],
         compiler_params=params(2),

time: 58 us -> 51.8 us (0.89)
  Pallas kernels: 57.1 us -> 50.9 us
    pallas_call x1, Pallas kernels: 13.7 us -> 9.36 us  [on_device(): pl.pallas_call(functools.partial(backward_kernel, n_rep), out_shape=(shap...]
    pallas_call x1, Pallas kernels: 16.9 us -> 15.3 us  [on_device(): pl.pallas_call(functools.partial(return_kernel, n_dom, n_rep), out_shape=...]
where the time goes in v3:
time: 51.8 us; the launch traced here: 51.6 us
  Pallas kernels  50.9 us (98%)
  between operations  0.67 us (1%)
    pallas_call x1, Pallas kernels, on_device(): pl.pallas_call(functools.partial(front_kernel, n_dom, n_rep), out_shape=(...  25.6 us
    pallas_call x1, Pallas kernels, on_device(): pl.pallas_call(functools.partial(return_kernel, n_dom, n_rep), out_shape=...  15.3 us
    pallas_call x1, Pallas kernels, on_device(): pl.pallas_call(functools.partial(backward_kernel, n_rep), out_shape=(shap...  9.36 us

profile of v3, /device:TPU:1, one launch (start us, length us, event | category | flops | bytes accessed | tf_op | source)
XLA Modules:
  0.0 51.6 jit_solution(9500220686709937652)
XLA Ops:
  0.6 25.6 %front.1 = (bf16[6,8,128,256]{3,2,1,0:T(8,128)(2,1)S(1)}, f32[6,3,128]{2,1,0:T(4,128)S(1)}, f32[48,128,128]{2,1,0:T(8,128)S(1)}, bf16[256,256]{1,0:T(8,128)(2,1)...) custom-call(bf16[256,256]{1,0:T(8,128)(2,1)} %feat_h.1, ...), custom_call_target="tpu_custom_call" | custom-call | tf_op jit(solution)/shard_map/front/pallas_call | solution.py:467
  26.2 0.0 copy-start
  26.3 9.4 %backward_pairs.1 = (bf16[6,2,128,128]{3,2,1,0:T(8,128)(2,1)S(1)}, f32[6,16,128]{2,1,0:T(8,128)S(1)}, f32[8,32,64]{2,1,0:T(8,128)S(1)}) custom-call(f32[8]{0:T(128)} %decay_h.3, s32[48]{0:T(128)} %home_h.3, s32[48]{0:T(128)} %other_h.3, s32[48]{0:T(128)} %kind_h.3, s32[3,48]{1,0:T(4,128)} %image_h.3, f32[6,3,128]{2,1,0:T(4,128)S(1)} %get-tuple-element.18.tiles, ...), custom_call_target="tpu_custom_call" | custom-call | tf_op jit(solution)/shard_map/backward_pairs/pallas_call | solution.py:491
  35.6 0.0 copy-done
  35.6 15.3 %return_gradients.1 = (bf16[256,256]{1,0:T(8,128)(2,1)S(1)}, f32[3,256]{1,0:T(4,128)S(1)}, f32[6,256]{1,0:T(8,128)S(1)}, f32[32,64]{1,0:T(8,128)S(1)}) custom-call(bf16[6,2,128,128]{3,2,1,0:T(8,128)(2,1)S(1)} %get-tuple-element.25.gfeat, f32[6,16,128]{2,1,0:T(8,128)S(1)} %get-tuple-element.26.side, f32[8,32,64]{2,1,0:T(8,128)S(1)} %get-tuple-element.27.mix, ...), custom_call_target="tpu_custom_call" | custom-call | tf_op jit(solution)/shard_map/return_gradients/pallas_call | solution.py:509
  50.9 0.7 %copy_out.1 = (bf16[256,256]{1,0:T(8,128)(2,1)}, f32[3,256]{1,0:T(4,128)}, f32[6,256]{1,0:T(8,128)}, f32[32,64]{1,0:T(8,128)}) custom-call(bf16[256,256]{1,0:T(8,128)(2,1)S(1)} %get-tuple-element.28.a, f32[3,256]{1,0:T(4,128)S(1)} %get-tuple-element.29.b, f32[6,256]{1,0:T(8,128)S(1)} %get-tuple-element.30.c, f32[32,64]{1,0:T(8,128)S(1)} %get-tuple-element.31.d), custom_call_target="tpu_custom_call" | custom-call | tf_op jit(solution)/shard_map/copy_out/pallas_call | solution.py:527
Async XLA Ops:
  26.2 9.4 %copy-start = (s32[4,128]{1,0:T(4,128)S(1)}, s32[4,128]{1,0:T(4,128)}, u32[]{:S(2)}) copy-start(s32[4,128]{1,0:T(4,128)} %rows.1) | copy-start | bytes 6148

commit v4 on v3

--- a/solution.py
+++ b/solution.py
@@ -12,6 +12,7 @@
 CELL = 2.0
 GROUP = 4
 BACK_GROUP = 8
+WIDE = 8
 F32 = jnp.float32
 BF16 = jnp.bfloat16
 MESH = pl.DeviceIdType.MESH
@@ -42,7 +43,7 @@
 def front_kernel(n_dom, n_rep, feat_h, pos_h, rows_h, radial_h, mixing_h, readout_h, decay_h, home_h, other_h,
                  kind_h, image_h, mapped, tiles, kern_t, packed, slope, adjoint, radial,
                  feat, pos, rows, mixing, readout, decay, home, other, kind, image,
-                 sendf, sendp, recvf, recvp, col, acc, msg, recv, pk, sl,
+                 sendf, sendp, recvf, recvp, col, kern_f, acc, msg, recv, pk, sl,
                  load, sf, sp, rf, rp, s4, r4, s5, r5, s1, r1, s2, r2, s3, r3):
     d = lax.axis_index("dom")
     r = lax.axis_index("rep")
@@ -67,21 +68,21 @@
     for copy in loads[:3]:
         copy.wait()
     copies = []
-    for q, o in enumerate(steps):
-        t = 2 * c + q
-        hot = (iota == rows[pl.ds(t, 1), :]).astype(F32)
-        sendf[q] = tn(hot.astype(BF16), feat[...]).astype(BF16)
+    hots = []
+    for q in range(2):
+        hot = (iota == rows[pl.ds(2 * c + q, 1), :]).astype(F32)
+        hots.append(hot.astype(BF16))
         sendp[q] = jnp.dot(pos[...], hot, precision=lax.Precision.HIGHEST, preferred_element_type=F32)
-        if q == 0:
-            pl.semaphore_wait(barrier, 2 + n_rep - 1)
-        to = {"dom": lax.rem(d + o + n_dom, n_dom), "rep": r}
-        cf = pltpu.make_async_remote_copy(sendf.at[q], recvf.at[t], sf.at[q], rf.at[t],
-                                          device_id=to, device_id_type=MESH)
-        cp = pltpu.make_async_remote_copy(sendp.at[q], recvp.at[t], sp.at[q], rp.at[t],
-                                          device_id=to, device_id_type=MESH)
-        cf.start()
-        cp.start()
-        copies += [cf, cp]
+    pl.semaphore_wait(barrier, 2 + n_rep - 1)
+    targets = [{"dom": lax.rem(d + o + n_dom, n_dom), "rep": r} for o in steps]
+    for src, dst, ss, rs in ((sendp, recvp, sp, rp), (sendf, recvf, sf, rf)):
+        for q in range(2):
+            t = 2 * c + q
+            if src is sendf:
+                sendf[q] = tn(hots[q], feat[...]).astype(BF16)
+            copies.append(pltpu.make_async_remote_copy(src.at[q], dst.at[t], ss.at[q], rs.at[t],
+                                                       device_id=targets[q], device_id_type=MESH))
+            copies[-1].start()
 
     def columns(j):
         for c in range(3):
@@ -106,51 +107,63 @@
         mapped[own + base, k] = res[:TILE]
         mapped[own + base + 1, k] = res[TILE:]
 
-    def unpack(base):
+    def spread(base):
+        lax.fori_loop(0, radial.shape[0], lambda k, _: (distant(base, k), 0)[1], 0)
+
+    relays = []
+
+    def relay(buf, first, ss, rs):
         for q in range(2):
-            tiles[own + base + q] = recvp[base + q]
-            columns(own + base + q)
-        lax.fori_loop(0, radial.shape[0], lambda k, _: (distant(base, k), 0)[1], 0)
-
-    relays = []
-    for q in range(2):
-        t = 2 * c + q
-        copies[2 * q].wait_recv()
-        copies[2 * q + 1].wait_recv()
-        relays.append(pltpu.make_async_remote_copy(recvf.at[t], recvf.at[t], s4.at[q], r4.at[t],
-                                                   device_id=partner, device_id_type=MESH))
-        relays.append(pltpu.make_async_remote_copy(recvp.at[t], recvp.at[t], s5.at[q], r5.at[t],
-                                                   device_id=partner, device_id_type=MESH))
-        relays[-2].start()
-        relays[-1].start()
-    unpack(2 * c)
-    for q in range(2):
-        t = 2 * (1 - c) + q
-        for dst, ss, rs in ((recvf.at[t], s4.at[q], r4.at[t]), (recvp.at[t], s5.at[q], r5.at[t])):
-            pltpu.make_async_remote_copy(dst, dst, ss, rs, device_id=partner, device_id_type=MESH).wait_recv()
-    unpack(2 * (1 - c))
-
-    acc[...] = jnp.zeros_like(acc)
+            t = 2 * c + q
+            copies[first + q].wait_recv()
+            relays.append(pltpu.make_async_remote_copy(buf.at[t], buf.at[t], ss.at[q], rs.at[t],
+                                                       device_id=partner, device_id_type=MESH))
+            relays[-1].start()
+
+    def relayed(buf, ss, rs):
+        for q in range(2):
+            t = 2 * (1 - c) + q
+            pltpu.make_async_remote_copy(buf.at[t], buf.at[t], ss.at[q], rs.at[t],
+                                         device_id=partner, device_id_type=MESH).wait_recv()
+
     pairs = home.shape[0]
-
-    def forward(g, _):
-        left, right = [], []
+    steps_all = pairs // GROUP
+
+    def kernels(g, _):
         for u in range(GROUP):
             p = g * GROUP + u
             h, o, k = home[p], other[p], kind[p]
             row = tiles[o]
             d2 = None
-            for c in range(3):
-                sep = (row[c:c + 1, :] + image[c, p].astype(F32) * CELL) - col[h, c]
+            for x in range(3):
+                sep = (row[x:x + 1, :] + image[x, p].astype(F32) * CELL) - col[h, x]
                 d2 = sep * sep if d2 is None else d2 + sep * sep
             kern = jnp.exp(d2 * (-decay[k]))
-            left.append(jnp.concatenate(
-                [(kern * (h == i).astype(F32)).astype(BF16) for i in range(own)], axis=0))
-            right.append(mapped[o, k])
+            for i in range(own):
+                kern_f[p, i * TILE:(i + 1) * TILE, :] = (kern * (h == i).astype(F32)).astype(BF16)
+        return 0
+
+    relay(recvp, 0, s5, r5)
+    relayed(recvp, s5, r5)
+    for t in range(4):
+        tiles[own + t] = recvp[t]
+        columns(own + t)
+    lax.fori_loop(0, steps_all // 2, kernels, 0)
+    relay(recvf, 2, s4, r4)
+    lax.fori_loop(steps_all // 2, steps_all, kernels, 0)
+    spread(2 * c)
+    relayed(recvf, s4, r4)
+    spread(2 * (1 - c))
+
+    acc[...] = jnp.zeros_like(acc)
+
+    def forward(g, _):
+        left = [kern_f[g * WIDE + u] for u in range(WIDE)]
+        right = [mapped[other[g * WIDE + u], kind[g * WIDE + u]] for u in range(WIDE)]
         acc[...] += mm(jnp.concatenate(left, axis=1), jnp.concatenate(right, axis=0))
         return 0
 
-    lax.fori_loop(0, pairs // GROUP, forward, 0)
+    lax.fori_loop(0, pairs // WIDE, forward, 0)
     share = atoms // n_rep
     for q in range(n_rep):
         msg[q] = acc[q * share:(q + 1) * share, :].astype(BF16)
@@ -478,7 +491,8 @@
             pltpu.VMEM(mixing.shape, BF16), pltpu.VMEM(readout_row.shape, F32), *pair_tables(),
             pltpu.VMEM((2, TILE, channels), BF16), pltpu.VMEM((2, 3, TILE), F32),
             pltpu.VMEM((4, TILE, channels), BF16), pltpu.VMEM((4, 3, TILE), F32),
-            pltpu.VMEM((n_ext, 3, TILE, TILE), F32), pltpu.VMEM((atoms, channels), F32),
+            pltpu.VMEM((n_ext, 3, TILE, TILE), F32),
+            pltpu.VMEM((pair_home.shape[0], atoms, TILE), BF16), pltpu.VMEM((atoms, channels), F32),
             *[pltpu.VMEM((n_rep, share, channels), BF16)] * 4,
             dma((11,)), *[dma((4,)) for _ in range(8)], *[dma((n_rep,)) for _ in range(6)],
         ],

time: 51.8 us -> 51.3 us (level)
  no operation moved by 1% of the time
where the time goes in v4:
time: 51.3 us; the launch traced here: 51.2 us
  Pallas kernels  50.5 us (98%)
  between operations  0.67 us (1%)
    pallas_call x1, Pallas kernels, on_device(): pl.pallas_call(functools.partial(front_kernel, n_dom, n_rep), out_shape=(...  25.1 us
    pallas_call x1, Pallas kernels, on_device(): pl.pallas_call(functools.partial(return_kernel, n_dom, n_rep), out_shape=...  15.3 us
    pallas_call x1, Pallas kernels, on_device(): pl.pallas_call(functools.partial(backward_kernel, n_rep), out_shape=(shap...  9.36 us

profile of v4, /device:TPU:1, one launch (start us, length us, event | category | flops | bytes accessed | tf_op | source)
XLA Modules:
  0.0 51.2 jit_solution(7482965265474051659)
XLA Ops:
  0.6 25.1 %front.1 = (bf16[6,8,128,256]{3,2,1,0:T(8,128)(2,1)S(1)}, f32[6,3,128]{2,1,0:T(4,128)S(1)}, f32[48,128,128]{2,1,0:T(8,128)S(1)}, bf16[256,256]{1,0:T(8,128)(2,1)...) custom-call(bf16[256,256]{1,0:T(8,128)(2,1)} %feat_h.1, ...), custom_call_target="tpu_custom_call" | custom-call | tf_op jit(solution)/shard_map/front/pallas_call | solution.py:480
  25.8 0.0 copy-start
  25.8 9.4 %backward_pairs.1 = (bf16[6,2,128,128]{3,2,1,0:T(8,128)(2,1)S(1)}, f32[6,16,128]{2,1,0:T(8,128)S(1)}, f32[8,32,64]{2,1,0:T(8,128)S(1)}) custom-call(f32[8]{0:T(128)} %decay_h.3, s32[48]{0:T(128)} %home_h.3, s32[48]{0:T(128)} %other_h.3, s32[48]{0:T(128)} %kind_h.3, s32[3,48]{1,0:T(4,128)} %image_h.3, f32[6,3,128]{2,1,0:T(4,128)S(1)} %get-tuple-element.18.tiles, ...), custom_call_target="tpu_custom_call" | custom-call | tf_op jit(solution)/shard_map/backward_pairs/pallas_call | solution.py:505
  35.2 0.0 copy-done
  35.2 15.3 %return_gradients.1 = (bf16[256,256]{1,0:T(8,128)(2,1)S(1)}, f32[3,256]{1,0:T(4,128)S(1)}, f32[6,256]{1,0:T(8,128)S(1)}, f32[32,64]{1,0:T(8,128)S(1)}) custom-call(bf16[6,2,128,128]{3,2,1,0:T(8,128)(2,1)S(1)} %get-tuple-element.25.gfeat, f32[6,16,128]{2,1,0:T(8,128)S(1)} %get-tuple-element.26.side, f32[8,32,64]{2,1,0:T(8,128)S(1)} %get-tuple-element.27.mix, ...), custom_call_target="tpu_custom_call" | custom-call | tf_op jit(solution)/shard_map/return_gradients/pallas_call | solution.py:523
  50.5 0.7 %copy_out.1 = (bf16[256,256]{1,0:T(8,128)(2,1)}, f32[3,256]{1,0:T(4,128)}, f32[6,256]{1,0:T(8,128)}, f32[32,64]{1,0:T(8,128)}) custom-call(bf16[256,256]{1,0:T(8,128)(2,1)S(1)} %get-tuple-element.28.a, f32[3,256]{1,0:T(4,128)S(1)} %get-tuple-element.29.b, f32[6,256]{1,0:T(8,128)S(1)} %get-tuple-element.30.c, f32[32,64]{1,0:T(8,128)S(1)} %get-tuple-element.31.d), custom_call_target="tpu_custom_call" | custom-call | tf_op jit(solution)/shard_map/copy_out/pallas_call | solution.py:541
Async XLA Ops:
  25.8 9.4 %copy-start = (s32[4,128]{1,0:T(4,128)S(1)}, s32[4,128]{1,0:T(4,128)}, u32[]{:S(2)}) copy-start(s32[4,128]{1,0:T(4,128)} %rows.1) | copy-start | bytes 6148

commit v5 on v4

--- a/solution.py
+++ b/solution.py
@@ -11,7 +11,7 @@
 OFFSETS = (1, -1, 2, -2)
 CELL = 2.0
 GROUP = 4
-BACK_GROUP = 8
+BACK_GROUP = 12
 WIDE = 8
 F32 = jnp.float32
 BF16 = jnp.bfloat16

time: 51.3 us -> 50.9 us (level)
  no operation moved by 1% of the time
where the time goes in v5:
time: 50.9 us; the launch traced here: 50.7 us
  Pallas kernels  50.1 us (98%)
  between operations  0.67 us (1%)
    pallas_call x1, Pallas kernels, on_device(): pl.pallas_call(functools.partial(front_kernel, n_dom, n_rep), out_shape=(...  25.1 us
    pallas_call x1, Pallas kernels, on_device(): pl.pallas_call(functools.partial(return_kernel, n_dom, n_rep), out_shape=...  15.3 us
    pallas_call x1, Pallas kernels, on_device(): pl.pallas_call(functools.partial(backward_kernel, n_rep), out_shape=(shap...  8.91 us

profile of v5, /device:TPU:1, one launch (start us, length us, event | category | flops | bytes accessed | tf_op | source)
XLA Modules:
  0.0 50.7 jit_solution(16162524913796425888)
XLA Ops:
  0.6 25.1 %front.1 = (bf16[6,8,128,256]{3,2,1,0:T(8,128)(2,1)S(1)}, f32[6,3,128]{2,1,0:T(4,128)S(1)}, f32[48,128,128]{2,1,0:T(8,128)S(1)}, bf16[256,256]{1,0:T(8,128)(2,1)...) custom-call(bf16[256,256]{1,0:T(8,128)(2,1)} %feat_h.1, ...), custom_call_target="tpu_custom_call" | custom-call | tf_op jit(solution)/shard_map/front/pallas_call | solution.py:480
  25.8 0.0 copy-start
  25.8 8.9 %backward_pairs.1 = (bf16[6,2,128,128]{3,2,1,0:T(8,128)(2,1)S(1)}, f32[6,16,128]{2,1,0:T(8,128)S(1)}, f32[8,32,64]{2,1,0:T(8,128)S(1)}) custom-call(f32[8]{0:T(128)} %decay_h.3, s32[48]{0:T(128)} %home_h.3, s32[48]{0:T(128)} %other_h.3, s32[48]{0:T(128)} %kind_h.3, s32[3,48]{1,0:T(4,128)} %image_h.3, f32[6,3,128]{2,1,0:T(4,128)S(1)} %get-tuple-element.18.tiles, ...), custom_call_target="tpu_custom_call" | custom-call | tf_op jit(solution)/shard_map/backward_pairs/pallas_call | solution.py:505
  34.7 0.0 copy-done
  34.7 15.3 %return_gradients.1 = (bf16[256,256]{1,0:T(8,128)(2,1)S(1)}, f32[3,256]{1,0:T(4,128)S(1)}, f32[6,256]{1,0:T(8,128)S(1)}, f32[32,64]{1,0:T(8,128)S(1)}) custom-call(bf16[6,2,128,128]{3,2,1,0:T(8,128)(2,1)S(1)} %get-tuple-element.25.gfeat, f32[6,16,128]{2,1,0:T(8,128)S(1)} %get-tuple-element.26.side, f32[8,32,64]{2,1,0:T(8,128)S(1)} %get-tuple-element.27.mix, ...), custom_call_target="tpu_custom_call" | custom-call | tf_op jit(solution)/shard_map/return_gradients/pallas_call | solution.py:523
  50.0 0.7 %copy_out.1 = (bf16[256,256]{1,0:T(8,128)(2,1)}, f32[3,256]{1,0:T(4,128)}, f32[6,256]{1,0:T(8,128)}, f32[32,64]{1,0:T(8,128)}) custom-call(bf16[256,256]{1,0:T(8,128)(2,1)S(1)} %get-tuple-element.28.a, f32[3,256]{1,0:T(4,128)S(1)} %get-tuple-element.29.b, f32[6,256]{1,0:T(8,128)S(1)} %get-tuple-element.30.c, f32[32,64]{1,0:T(8,128)S(1)} %get-tuple-element.31.d), custom_call_target="tpu_custom_call" | custom-call | tf_op jit(solution)/shard_map/copy_out/pallas_call | solution.py:541
Async XLA Ops:
  25.8 8.9 %copy-start = (s32[4,128]{1,0:T(4,128)S(1)}, s32[4,128]{1,0:T(4,128)}, u32[]{:S(2)}) copy-start(s32[4,128]{1,0:T(4,128)} %rows.1) | copy-start | bytes 6148
